TPU v7x, 256 devices: a whole 4x4x8 slice. The times are simulated.
256 devices in a mesh: site: 64 (over x, z, core), slab: 4 (over y).
Axes of the slice: x: 4, y: 4, z: 8, core: 2. Of those that a mesh axis runs over, the one named last changes fastest.
Arguments:
- jacobian: float32 [32768, 16384], P('site', 'slab'), may hold values from -3000 to 3000, as said below
- probe: float32 [16384, 256], P('slab'), may hold values from -0.046875 to 0.046875
Outputs:
- basis: float32 [32768, 256], P('site')
- projected: float32 [256, 16384], P('site', 'slab')
Inputs may be any that keep to these rules, and one draw needn't show every extreme that they name: `jacobian`: finite real sensitivities.
All inputs are finite; a program needn't handle non-finite values.
Results may differ from a plain program's by a relative error of at most 0.00028.
Values sent between devices are 32-bit elements; how exact they have to be, the bound alone decides.
No kernel may reach another device: no remote copies, remote signals or barrier semaphores. Data moves between devices by JAX's collectives and lax.ppermute only.
A program may use at most 64 MiB of HBM per device.

v0:
```python
import jax
import jax.numpy as jnp
from jax import lax
from jax.sharding import PartitionSpec as P


def local_product(left, right):
    return jnp.dot(left, right, preferred_element_type=jnp.float32, precision=lax.Precision.HIGHEST)


def shards(jacobian, probe):
    row_count = jacobian.shape[0]
    width = probe.shape[1]
    total_rows = row_count * lax.axis_size("site")
    partial_value = local_product(jacobian, probe)
    sketch = lax.psum(partial_value, "slab")
    gram = lax.psum(local_product(sketch.T, sketch), "site")
    lower = jnp.linalg.cholesky(gram)
    ortho = jax.scipy.linalg.solve_triangular(lower, sketch.T, lower=True).T
    basis = jnp.sqrt(jnp.float32(total_rows)) * ortho
    owned = width // lax.axis_size("site")
    local_terms = local_product(ortho.T, jacobian)
    full_sum = lax.psum(local_terms, "site")
    projected = lax.dynamic_slice_in_dim(full_sum, lax.axis_index("site") * owned, owned, 0)
    return (basis, projected)


def solution(mesh):
    return jax.shard_map(
        shards,
        mesh=mesh,
        in_specs=(P("site", "slab"), P("slab", None)),
        out_specs=(P("site", None), P("site", "slab")),
        check_vma=False,
    )
```

profile of v0, /device:TPU:8, one launch (start us, length us, event | category | flops | bytes accessed | tf_op | source)
XLA Modules:
  0.0 527.4 jit_solution(14197104399093029755)
XLA Ops:
  7.2 0.0 all-reduce.5.cloned.1.call-start
  7.2 10.6 %fusion.11 = f32[512,256]{1,0:T(8,128)} fusion(f32[512,4096]{1,0:T(8,128)} %param.2, f32[4096,256]{1,0:T(8,128)} %param.3), kind=kOutput, calls=%fused_computation.33 | convolution fusion | flops 6442450944 | bytes 13107200 | tf_op jit(solution)/shard_map/dot_general | solution.py:8
  17.8 0.0 all-reduce.7.cloned.1.call-start
  17.8 50.2 %all-reduce.5.cloned.1.call-done = f32[512,256]{1,0:T(8,128)} async-done(((f32[512,256]{1,0:T(8,128)}), f32[512,256]{1,0:T(8,128)}) %all-reduce.5.cloned.1.call-update) | async-done | bytes 524304 | tf_op jit(solution)/shard_map/psum | solution.py:16
  68.0 3.0 fusion.12
  71.0 0.0 all-reduce.7.cloned.1.call-update
  71.0 0.2 all-reduce.9.cloned.1.call-start
  71.3 178.5 %all-reduce.7.cloned.1.call-done = f32[256,256]{0,1:T(8,128)} async-done(((f32[256,256]{0,1:T(8,128)}), f32[256,256]{0,1:T(8,128)}) %all-reduce.7.cloned.1.call-update) | async-done | bytes 262160 | tf_op jit(solution)/shard_map/psum | solution.py:17
  249.7 1.1 copy.5
  250.8 1.0 fusion.3
  251.8 11.7 %cholesky.50 = f32[128,128]{1,0:T(8,128)S(1)} custom-call(f32[128,128]{1,0:T(8,128)S(1)} %cholesky.118), custom_call_target="Cholesky" | custom-call | tf_op jit(solution)/shard_map/jit(cholesky)/cholesky | solution.py:18
  263.6 9.8 %custom-call.15 = f32[1,128,128]{1,2,0:T(8,128)S(1)} custom-call(f32[1,128,128]{2,1,0:T(8,128)S(1)} %get-tuple-element.25), custom_call_target="InvertDiagBlocksLowerTriangular" | custom-call | tf_op jit(solution)/shard_map/jit(cholesky)/cholesky | solution.py:18
  273.4 0.2 constant_dynamic-update-slice_fusion
  273.6 0.3 convolution_subtract_fusion.1
  273.9 11.7 %cholesky.105 = f32[128,128]{1,0:T(8,128)S(1)} custom-call(f32[128,128]{1,0:T(8,128)S(1)} %convolution_subtract_fusion.1), custom_call_target="Cholesky" | custom-call | tf_op jit(solution)/shard_map/jit(cholesky)/cholesky | solution.py:18
  285.7 0.7 compare_reduce_fusion
  287.8 0.1 triangular_solve.57
  287.8 4.3 while.1
  288.0 0.6 fusion.23
  288.6 1.4 bitcast_dynamic-update-slice_fusion.2
  290.1 0.6 fusion.23
  290.7 1.4 bitcast_dynamic-update-slice_fusion.2
  292.1 19.7 %custom-call.16 = f32[2,128,128]{1,2,0:T(8,128)S(1)} custom-call(f32[2,128,128]{2,1,0:T(8,128)S(1)} %get-tuple-element.9), custom_call_target="InvertDiagBlocksLowerTriangular" | custom-call | tf_op jit(solution)/shard_map/jit(_solve_triangular)/triangular_solve | solution.py:19
  311.8 0.4 fusion.1
  312.2 0.6 convolution_subtract_fusion
  312.8 0.4 fusion.5
  313.3 10.9 %fusion = f32[256,4096]{1,0:T(8,128)} fusion(f32[512,4096]{1,0:T(8,128)} %param.2, f32[128,512]{1,0:T(8,128)S(1)} %fusion.5, f32[128,512]{1,0:T(8,128)S(1)} %fusion.1), kind=kOutput, calls=%fused_computation.6 | convolution fusion | flops 6442582016 | bytes 13107200 | tf_op jit(solution)/shard_map/dot_general | solution.py:8
  324.2 0.0 all-reduce.9.cloned.1.call-update
  324.2 0.1 multiply_bitcast_fusion
  324.3 1.0 copy.6
  325.3 194.0 %all-reduce.9.cloned.1.call-done = f32[256,4096]{1,0:T(8,128)} async-done(((f32[256,4096]{1,0:T(8,128)}), f32[256,4096]{1,0:T(8,128)}) %all-reduce.9.cloned.1.call-update) | async-done | bytes 4194320 | tf_op jit(solution)/shard_map/psum | solution.py:23
  519.3 1.5 constant_dynamic-slice_fusion.1
  (12 shorter events, 0.2 us)
Async XLA Ops:
  7.2 60.9 %all-reduce.5.cloned.1.call-start = ((), (), s32[]{:S(2)}) async-start(), calls=%async_computation | async-start | bytes 1048576 | tf_op jit(solution)/shard_map/psum | solution.py:16
  17.8 232.0 %all-reduce.7.cloned.1.call-start = ((), (), s32[]{:S(2)}) async-start(), calls=%async_computation.1 | async-start | bytes 524288 | tf_op jit(solution)/shard_map/psum | solution.py:17
  68.0 243.8 %copy-start = (f32[512,256]{1,0:T(8,128)S(1)}, f32[512,256]{1,0:T(8,128)}, u32[]{:S(2)}) copy-start(f32[512,256]{1,0:T(8,128)} %all-reduce.5.cloned.1.call-done) | copy-start | bytes 1572868
  71.0 448.3 %all-reduce.9.cloned.1.call-start = ((), (), s32[]{:S(2)}) async-start(), calls=%async_computation.2 | async-start | bytes 8388608 | tf_op jit(solution)/shard_map/psum | solution.py:23
Sparse Core Ops, SparseCore 0:
  17.9 50.0 all-reduce.4
  72.1 177.5 all-reduce.6
  324.4 194.8 all-reduce.8
where the time goes:
time: 528 us; the launch traced here: 527 us
  waiting for transfers between devices  423 us (80%)
  other arithmetic  54.8 us (10%)
  matrix products  26.4 us (5%)
  between operations  15.2 us (3%)
  local copies, waits for them, and re-layouts  7.78 us (1%)
    psum x1, waiting for transfers between devices, shards(): full_sum = lax.psum(local_terms, 'site')  194 us
    psum x1, waiting for transfers between devices, shards(): gram = lax.psum(local_product(sketch.T, sketch), 'site')  178 us
    psum x1, waiting for transfers between devices, shards(): sketch = lax.psum(partial_value, 'slab')  50.2 us
    another operation x6, other arithmetic, shards(): lower = jnp.linalg.cholesky(gram)  34 us
    dot_general x3, matrix products, local_product(): jnp.dot(left, right, preferred_element_type=jnp.float32, precision=lax.Pr...  24.5 us
    another operation x3, other arithmetic, shards(): ortho = jax.scipy.linalg.solve_triangular(lower, sketch.T, lower=True).T  19.7 us
  transfers between devices with their start and end apart: 3, of which 3 were waited for; matrix products, arithmetic and copies ran while one was open for 0% of the time, Pallas kernels for 0%

commit v1 on v0

v1 whole, which is shorter than its diff:
```python
import functools

import jax
import jax.numpy as jnp
from jax import lax
from jax.experimental import pallas as pl
from jax.experimental.pallas import tpu as pltpu
from jax.sharding import Mesh
from jax.sharding import PartitionSpec as P

HIGH = lax.Precision.HIGH
HIGHEST = lax.Precision.HIGHEST
BLOCK = 128


def pairs(size, mask):
    return [(i, i ^ mask) for i in range(size)]


def swap(value, axis, mask):
    return lax.ppermute(value, axis, pairs(lax.axis_size(axis), mask))


def reciprocal(value):
    guess = pl.reciprocal(value, approx=True)
    guess = guess * (2.0 - value * guess)
    return guess * (2.0 - value * guess)


def eliminate(square):
    size = square.shape[0]
    wide = 2 * size
    count = size // 8
    same = lax.broadcasted_iota(jnp.int32, (size, size), 0) == lax.broadcasted_iota(jnp.int32, (size, size), 1)
    joined = jnp.concatenate([square, same.astype(jnp.float32)], axis=1)
    tiles = [joined[8 * i : 8 * i + 8] for i in range(count)]
    place = lax.broadcasted_iota(jnp.int32, (8, wide), 0)
    done = []
    for q in range(count):
        columns = [
            [jnp.broadcast_to(tiles[i][:, 8 * q + k : 8 * q + k + 1], (8, wide)) for i in range(q, count)]
            for k in range(8)
        ]
        pivots = None
        for k in range(8):
            pivot = jnp.broadcast_to(columns[k][0][k : k + 1], (8, wide))
            pivots = pivot if pivots is None else jnp.where(place >= k, pivot, pivots)
            inverse = reciprocal(pivot)
            factor = [c * inverse for c in columns[k]]
            factor[0] = jnp.where(place > k, factor[0], 0.0)
            for m in range(k + 1, 8):
                edge = jnp.broadcast_to(columns[m][0][k : k + 1], (8, wide))
                columns[m] = [c - f * edge for c, f in zip(columns[m], factor)]
            row = jnp.broadcast_to(tiles[q][k : k + 1], (8, wide))
            for i in range(q, count):
                tiles[i] = tiles[i] - factor[i - q] * row
        done.append(tiles[q] * lax.rsqrt(pivots))
    return jnp.concatenate([d[:, size:] for d in done], axis=0)


def factor_kernel(place_ref, *refs):
    parts, (whole_ref, split_ref, gram) = refs[:-3], refs[-3:]
    place = place_ref[0]
    rows, size = parts[0].shape
    for k, part in enumerate(parts):
        start = pl.multiple_of(jnp.bitwise_xor(place, k) * rows, rows)
        gram[pl.ds(start, rows), :] = part[...]
    blocks = size // BLOCK
    column = lax.broadcasted_iota(jnp.int32, (BLOCK, size), 1)
    row = lax.broadcasted_iota(jnp.int32, (BLOCK, size), 0)
    rest = [gram[BLOCK * i : BLOCK * (i + 1), :] for i in range(blocks)]
    for p in range(blocks):
        first = BLOCK * p
        inverse = eliminate(rest[p][:, first : first + BLOCK])
        inside = (column >= first) & (column < first + BLOCK)
        strip = jnp.where(inside, (column - first == row).astype(jnp.float32), rest[p])
        strip = jnp.dot(inverse, strip, precision=HIGHEST, preferred_element_type=jnp.float32)
        kept = jnp.where(column < first + BLOCK, strip, 0.0)
        whole_ref[first : first + BLOCK, :] = kept
        half = lax.broadcasted_iota(jnp.int32, (8, size), 0) < 4
        for t in range(BLOCK // 16):
            low, high = kept[16 * t : 16 * t + 8], kept[16 * t + 8 : 16 * t + 16]
            to = first // 2 + 8 * t
            split_ref[0, to : to + 8, :] = jnp.where(half, low, pltpu.roll(high, 4, 0))
            split_ref[1, to : to + 8, :] = jnp.where(half, pltpu.roll(low, 4, 0), high)
        if p + 1 < blocks:
            change = lax.dot_general(
                strip[:, first + BLOCK :],
                strip,
                (((0,), (0,)), ((), ())),
                precision=HIGHEST,
                preferred_element_type=jnp.float32,
            )
            for i in range(p + 1, blocks):
                at = BLOCK * (i - p - 1)
                rest[i] = jnp.where(inside, 0.0, rest[i]) - change[at : at + BLOCK]


def inverse_factor(parts, place):
    rows, size = parts[0].shape
    vmem = pl.BlockSpec(memory_space=pltpu.VMEM)
    return pl.pallas_call(
        factor_kernel,
        out_shape=(
            jax.ShapeDtypeStruct((size, size), jnp.float32),
            jax.ShapeDtypeStruct((2, size // 2, size), jnp.float32),
        ),
        in_specs=[pl.BlockSpec(memory_space=pltpu.SMEM)] + [vmem] * len(parts),
        out_specs=(vmem, vmem),
        scratch_shapes=[pltpu.VMEM((size, size), jnp.float32)],
        cost_estimate=pl.CostEstimate(flops=4 * size**3 * 50, bytes_accessed=12 * size * size, transcendentals=size),
        name="inverse_factor",
    )(place, *parts)


def group_sum(value, axis):
    one, two, three = (swap(value, axis, k) for k in (1, 2, 3))
    return (value + one) + (two + three)


def shards(jacobian, probe):
    width = probe.shape[1]
    columns = jacobian.shape[1]
    nx, nz, nc, ns = (lax.axis_size(a) for a in ("x", "z", "core", "slab"))
    total_rows = jacobian.shape[0] * nx * nz * nc
    slab, core = lax.axis_index("slab"), lax.axis_index("core")

    partial_value = jnp.dot(jacobian, probe, precision=HIGH, preferred_element_type=jnp.float32)
    middle = jacobian.shape[0] // 2
    top, bottom = partial_value[:middle], partial_value[middle:]
    top, bottom = top + swap(top, "slab", 1), bottom + swap(bottom, "slab", 3)
    top, bottom = top + swap(top, "slab", 3), bottom + swap(bottom, "slab", 1)
    sketch = jnp.concatenate([top, bottom], axis=0)

    gram = jnp.dot(sketch.T, sketch, precision=HIGHEST, preferred_element_type=jnp.float32)
    part = lax.dynamic_slice_in_dim(gram, slab * (width // ns), width // ns, 0)
    part = part + swap(part, "core", 1)
    part = group_sum(part, "x")
    part = group_sum(part, "z")
    part = part + swap(part, "z", 7)
    parts = [part] + [swap(part, "slab", k) for k in range(1, ns)]

    terms = jnp.dot(sketch.T, jacobian, precision=HIGH, preferred_element_type=jnp.float32)
    terms = terms.reshape(nc, width // nc, nx, nz, columns // (nx * nz)).transpose(0, 2, 3, 1, 4)
    mine = lax.dynamic_index_in_dim(terms, core, 0, keepdims=False)
    other = lax.dynamic_index_in_dim(terms, 1 - core, 0, keepdims=False)
    mine = mine + swap(other, "core", 1)
    mine = lax.all_to_all(mine, "x", 0, 0).sum(0)
    mine = lax.all_to_all(mine, "z", 0, 0).sum(0)
    across = swap(mine, "core", 1)
    terms = jnp.where(core == 0, jnp.stack([mine, across]), jnp.stack([across, mine])).reshape(width, -1)

    whole, split = inverse_factor(parts, slab.reshape(1))
    basis = jnp.sqrt(jnp.float32(total_rows)) * lax.dot_general(
        sketch, whole, (((1,), (1,)), ((), ())), precision=HIGHEST, preferred_element_type=jnp.float32
    )
    rows = lax.dynamic_index_in_dim(split, core, 0, keepdims=False)
    owned = jnp.dot(rows, terms, precision=HIGHEST, preferred_element_type=jnp.float32)
    owned = owned.reshape(nx * nz, width // (nx * nz * nc), -1)
    owned = lax.all_to_all(owned, ("x", "z"), 0, 0)
    return basis, owned.transpose(1, 0, 2).reshape(owned.shape[1], columns)


def solution(mesh):
    grid = Mesh(mesh.devices.reshape(4, 8, 2, 4), ("x", "z", "core", "slab"))
    site = ("x", "z", "core")
    return jax.shard_map(
        shards,
        mesh=grid,
        in_specs=(P(site, "slab"), P("slab", None)),
        out_specs=(P(site, None), P(site, "slab")),
        check_vma=False,
    )
```

time: 528 us -> 148 us (0.28)
  waiting for transfers between devices: 423 us -> 65.7 us
  other arithmetic: 54.8 us -> 2.04 us
  starting transfers between devices: 0.3 us -> 42 us
  between operations: 15.2 us -> 0.84 us
  Pallas kernels: 0 us -> 12.5 us
  matrix products: 26.4 us -> 17.3 us
    psum x3 -> x0, waiting for transfers between devices: 423 us -> none  [the longest x1 194 us: shards(): full_sum = lax.psum(local_terms, 'site')]
    another operation x9 -> x0, other arithmetic: 53.7 us -> none  [the longest x6 34 us: shards(): lower = jnp.linalg.cholesky(gram)]
    ppermute x0 -> x17, waiting for transfers between devices: none -> 37.6 us  [swap(): return lax.ppermute(value, axis, pairs(lax.axis_size(axis), mask))]
    all_to_all x0 -> x3, waiting for transfers between devices: none -> 28.2 us  [the longest x1 20.5 us: shards(): mine = lax.all_to_all(mine, 'x', 0, 0).sum(0)]
    ppermute x0 -> x17, starting transfers between devices: none -> 23.5 us  [swap(): return lax.ppermute(value, axis, pairs(lax.axis_size(axis), mask))]
    all_to_all x0 -> x3, starting transfers between devices: none -> 18.6 us  [the longest x1 8.46 us: shards(): mine = lax.all_to_all(mine, 'z', 0, 0).sum(0)]
    pallas_call x0 -> x1, Pallas kernels: none -> 12.5 us  [inverse_factor(): pl.pallas_call(factor_kernel, out_shape=(jax.ShapeDtypeStruct((size, size...]
    dot_general x3 -> x5, matrix products: 24.5 us -> 17.3 us  [the longest x1 7.46 us: shards(): jnp.dot(jacobian, probe, precision=HIGH, preferred_element_type=jnp.float32)]
  transfers between devices with their start and end apart: 3 -> 20, of which waited for: 3 -> 14; matrix products, arithmetic and copies ran while one was open for 0% -> 4% of each run, Pallas kernels for 0% -> 9%
where the time goes in v1:
time: 148 us; the launch traced here: 146 us
  waiting for transfers between devices  65.7 us (44%)
  starting transfers between devices  42 us (28%)
  matrix products  17.3 us (12%)
  Pallas kernels  12.5 us (8%)
  local copies, waits for them, and re-layouts  5.25 us (4%)
  other arithmetic  2.04 us (1%)
    ppermute x17, waiting for transfers between devices, swap(): return lax.ppermute(value, axis, pairs(lax.axis_size(axis), mask))  37.6 us
    ppermute x17, starting transfers between devices, swap(): return lax.ppermute(value, axis, pairs(lax.axis_size(axis), mask))  23.5 us
    all_to_all x1, waiting for transfers between devices, shards(): mine = lax.all_to_all(mine, 'x', 0, 0).sum(0)  20.5 us
    pallas_call x1, Pallas kernels, inverse_factor(): pl.pallas_call(factor_kernel, out_shape=(jax.ShapeDtypeStruct((size, size...  12.5 us
    all_to_all x1, starting transfers between devices, shards(): mine = lax.all_to_all(mine, 'z', 0, 0).sum(0)  8.46 us
    all_to_all x1, waiting for transfers between devices, shards(): owned = lax.all_to_all(owned, ('x', 'z'), 0, 0)  7.65 us
    dot_general x1, matrix products, shards(): jnp.dot(jacobian, probe, precision=HIGH, preferred_element_type=jnp.float32)  7.46 us
    dot_general x1, matrix products, shards(): jnp.dot(sketch.T, jacobian, precision=HIGH, preferred_element_type=jnp.fl...  6.19 us
  transfers between devices with their start and end apart: 20, of which 14 were waited for; matrix products, arithmetic and copies ran while one was open for 4% of the time, Pallas kernels for 9%

profile of v1, /device:TPU:8, one launch (start us, length us, event | category | flops | bytes accessed | tf_op | source)
XLA Modules:
  0.0 145.7 jit_solution(5158786724407293233)
XLA Ops:
  0.6 7.5 %fusion.8 = f32[512,256]{1,0:T(8,128)S(1)} fusion(f32[512,4096]{1,0:T(8,128)} %param.2, f32[4096,256]{1,0:T(8,128)} %param.3), kind=kOutput, calls=%fused_computation.22 | convolution fusion | flops 3221225472 | bytes 13107200 | tf_op jit(solution)/shard_map/dot_general | solution.py:128
  8.1 2.2 %collective-permute-start = (f32[256,256]{1,0:T(8,128)S(1)}, f32[256,256]{1,0:T(8,128)S(1)}, u32[]{:S(2)}, u32[]{:S(2)}) collective-permute-start(f32[256,256]{1,0:T(8,128)S(1)} %get-tuple-element.10), channel_id=1, source_target_pairs={{0,1},{1,0},{2,3},{3,2},{4,5},{5,4},{6,7},{7,6},{8,9},{9,8},{10,11... | collective-permute-start | bytes 786440 | tf_op jit(solution)/shard_map/ppermute | solution.py:21
  11.1 5.2 %collective-permute-done = f32[256,256]{1,0:T(8,128)S(1)} collective-permute-done((f32[256,256]{1,0:T(8,128)S(1)}, f32[256,256]{1,0:T(8,128)S(1)}, u32[]{:S(2)}, u32[]{:S(2)}) %collective-permute-start) | collective-permute-done | bytes 262176 | tf_op jit(solution)/shard_map/ppermute | solution.py:21
  16.3 0.8 collective-permute-done.2
  17.2 1.8 %collective-permute-start.1 = (f32[256,256]{1,0:T(8,128)S(1)}, f32[256,256]{1,0:T(8,128)S(1)}, u32[]{:S(2)}, u32[]{:S(2)}) collective-permute-start(f32[256,256]{1,0:T(8,128)S(1)} %get-tuple-element.8), channel_id=1, source_target_pairs={{0,3},{1,2},{2,1},{3,0},{4,7},{5,6},{6,5},{7,4},{8,11},{9,10},{10,... | collective-permute-start | bytes 786440 | tf_op jit(solution)/shard_map/ppermute | solution.py:21
  19.0 2.6 %collective-permute-start.3 = (f32[256,256]{1,0:T(8,128)S(1)}, f32[256,256]{1,0:T(8,128)S(1)}, u32[]{:S(2)}, u32[]{:S(2)}) collective-permute-start(f32[256,256]{1,0:T(8,128)S(1)} %get-tuple-element.9), channel_id=1, source_target_pairs={{0,1},{1,0},{2,3},{3,2},{4,5},{5,4},{6,7},{7,6},{8,9},{9,8},{10,11... | collective-permute-start | bytes 786440 | tf_op jit(solution)/shard_map/ppermute | solution.py:21
  21.6 2.6 %collective-permute-done.1 = f32[256,256]{1,0:T(8,128)S(1)} collective-permute-done((f32[256,256]{1,0:T(8,128)S(1)}, f32[256,256]{1,0:T(8,128)S(1)}, u32[]{:S(2)}, u32[]{:S(2)}) %collective-permute-start.1) | collective-permute-done | bytes 262176 | tf_op jit(solution)/shard_map/ppermute | solution.py:21
  24.2 2.2 %collective-permute-done.3 = f32[256,256]{1,0:T(8,128)S(1)} collective-permute-done((f32[256,256]{1,0:T(8,128)S(1)}, f32[256,256]{1,0:T(8,128)S(1)}, u32[]{:S(2)}, u32[]{:S(2)}) %collective-permute-start.3) | collective-permute-done | bytes 262176 | tf_op jit(solution)/shard_map/ppermute | solution.py:21
  26.5 6.2 %convolution_bitcast_fusion = f32[32,8,32,128]{3,1,2,0:T(8,128)S(1)} fusion(f32[512,4096]{1,0:T(8,128)} %param.2, f32[256,256]{1,0:T(8,128)S(1)} %add.55, f32[256,256]{1,0:T(8,128)S(1)} %add.53), kind=kOutput, calls=%fused_computation | convolution fusion | flops 3221356544 | bytes 13107200 | tf_op jit(solution)/shard_map/dot_general | solution.py:143
  34.2 4.1 %collective-permute-done.15 = f32[4,8,128,128]{3,1,2,0:T(8,128)S(1)} collective-permute-done((f32[4,8,128,128]{3,1,2,0:T(8,128)S(1)}, f32[4,8,128,128]{3,1,2,0:T(8,128)S(1)}, u32[]{:S(2)}, u32[]{:S(2)}) %collective-permute-start.15) | collective-permute-done | bytes 2097184 | tf_op jit(solution)/shard_map/ppermute | solution.py:21
  38.3 1.7 %fusion = f32[4,8,128,128]{3,1,2,0:T(8,128)} fusion(f32[4,8,128,128]{3,1,2,0:T(8,128)S(1)} %collective-permute-done.15, f32[1,128,4,8,128]{4,3,2,1,0:T(8,128)S(1)} %get-tuple-element.6), kind=kLoop, calls=%fused_computation.3 | loop fusion | flops 524288 | bytes 6291456 | tf_op jit(solution)/shard_map/add | solution.py:147
  40.0 4.3 %all-to-all-start = ((f32[4,8,128,128]{3,1,2,0:T(8,128)}), f32[4,8,128,128]{3,1,2,0:T(8,128)S(1)}, u32[]{:S(2)}, u32[]{:S(2)}) async-start(f32[4,8,128,128]{3,1,2,0:T(8,128)} %fusion), calls=%async_computation | async-start | bytes 4194304 | tf_op jit(solution)/shard_map/all_to_all | solution.py:148
  44.3 1.0 fusion.1
  45.5 1.2 collective-permute-done.4
  46.7 2.1 %collective-permute-start.5 = (f32[64,256]{1,0:T(8,128)S(1)}, f32[64,256]{1,0:T(8,128)S(1)}, u32[]{:S(2)}, u32[]{:S(2)}) collective-permute-start(f32[64,256]{1,0:T(8,128)S(1)} %fusion.14), channel_id=1, source_target_pairs={{0,64},{64,0},{128,192},{192,128},{1,65},{65,1},{129,193},{193,129... | collective-permute-start | bytes 196616 | tf_op jit(solution)/shard_map/ppermute | solution.py:21
  48.8 2.7 %collective-permute-start.6 = (f32[64,256]{1,0:T(8,128)S(1)}, f32[64,256]{1,0:T(8,128)S(1)}, u32[]{:S(2)}, u32[]{:S(2)}) collective-permute-start(f32[64,256]{1,0:T(8,128)S(1)} %fusion.14), channel_id=1, source_target_pairs={{0,128},{64,192},{128,0},{192,64},{1,129},{65,193},{129,1},{193,65... | collective-permute-start | bytes 196616 | tf_op jit(solution)/shard_map/ppermute | solution.py:21
  51.6 20.5 %all-to-all-done = f32[4,8,128,128]{3,1,2,0:T(8,128)S(1)} async-done(((f32[4,8,128,128]{3,1,2,0:T(8,128)}), f32[4,8,128,128]{3,1,2,0:T(8,128)S(1)}, u32[]{:S(2)}, u32[]{:S(2)}) %all-to-all-start) | async-done | bytes 2097184 | tf_op jit(solution)/shard_map/all_to_all | solution.py:148
  72.2 0.9 copy.13
  73.1 8.5 %all-to-all-start.1 = ((f32[8,128,128]{2,1,0:T(8,128)}), f32[8,128,128]{2,1,0:T(8,128)S(1)}, u32[]{:S(2)}, u32[]{:S(2)}) async-start(f32[8,128,128]{2,1,0:T(8,128)} %copy.13), calls=%async_computation.1 | async-start | bytes 1048576 | tf_op jit(solution)/shard_map/all_to_all | solution.py:149
  81.6 3.9 %collective-permute-start.10 = (f32[64,256]{1,0:T(8,128)S(1)}, f32[64,256]{1,0:T(8,128)S(1)}, u32[]{:S(2)}, u32[]{:S(2)}) collective-permute-start(f32[64,256]{1,0:T(8,128)S(1)} %add_add_fusion.1), channel_id=1, source_target_pairs={{0,24},{8,16},{16,8},{24,0},{32,56},{40,48},{48,40},{56,32},{1,25}... | collective-permute-start | bytes 196616 | tf_op jit(solution)/shard_map/ppermute | solution.py:21
  86.2 11.1 %collective-permute-done.10 = f32[64,256]{1,0:T(8,128)S(1)} collective-permute-done((f32[64,256]{1,0:T(8,128)S(1)}, f32[64,256]{1,0:T(8,128)S(1)}, u32[]{:S(2)}, u32[]{:S(2)}) %collective-permute-start.10) | collective-permute-done | bytes 65568 | tf_op jit(solution)/shard_map/ppermute | solution.py:21
  97.3 2.5 %collective-permute-done.9 = f32[64,256]{1,0:T(8,128)S(1)} collective-permute-done((f32[64,256]{1,0:T(8,128)S(1)}, f32[64,256]{1,0:T(8,128)S(1)}, u32[]{:S(2)}, u32[]{:S(2)}) %collective-permute-start.9) | collective-permute-done | bytes 65568 | tf_op jit(solution)/shard_map/ppermute | solution.py:21
  99.8 2.8 %collective-permute-start.11 = (f32[64,256]{1,0:T(8,128)S(1)}, f32[64,256]{1,0:T(8,128)S(1)}, u32[]{:S(2)}, u32[]{:S(2)}) collective-permute-start(f32[64,256]{1,0:T(8,128)S(1)} %add_add_fusion), channel_id=1, source_target_pairs={{0,56},{8,48},{16,40},{24,32},{32,24},{40,16},{48,8},{56,0},{1,57}... | collective-permute-start | bytes 196616 | tf_op jit(solution)/shard_map/ppermute | solution.py:21
  102.6 3.4 %collective-permute-done.11 = f32[64,256]{1,0:T(8,128)S(1)} collective-permute-done((f32[64,256]{1,0:T(8,128)S(1)}, f32[64,256]{1,0:T(8,128)S(1)}, u32[]{:S(2)}, u32[]{:S(2)}) %collective-permute-start.11) | collective-permute-done | bytes 65568 | tf_op jit(solution)/shard_map/ppermute | solution.py:21
  106.1 1.8 %collective-permute-start.12 = (f32[64,256]{1,0:T(8,128)S(1)}, f32[64,256]{1,0:T(8,128)S(1)}, u32[]{:S(2)}, u32[]{:S(2)}) collective-permute-start(f32[64,256]{1,0:T(8,128)S(1)} %add.64.refs_0_), channel_id=1, source_target_pairs={{0,1},{1,0},{2,3},{3,2},{4,5},{5,4},{6,7},{7,6},{8,9},{9,8},{10,11... | collective-permute-start | bytes 196616 | tf_op jit(solution)/shard_map/ppermute | solution.py:21
  108.4 1.3 collective-permute-start.14
  110.5 3.2 %collective-permute-done.13.refs_2_ = f32[64,256]{1,0:T(8,128)S(1)} collective-permute-done((f32[64,256]{1,0:T(8,128)S(1)}, f32[64,256]{1,0:T(8,128)S(1)}, u32[]{:S(2)}, u32[]{:S(2)}) %collective-permute-start.13) | collective-permute-done | bytes 65568 | tf_op jit(solution)/shard_map/ppermute | solution.py:21
  114.4 12.5 %inverse_factor.1 = (f32[256,256]{1,0:T(8,128)}, f32[2,128,256]{2,1,0:T(8,128)}) custom-call(s32[1]{0:T(128)} %bitcast.place_ref, f32[64,256]{1,0:T(8,128)} %copy-done, f32[64,256]{1,0:T(8,128)} %copy-done.1, f32[64,256]{1,0:T(8,128)} %copy-done.2, f32[64,256]{1,0:T(8,128)} %copy-done.3), custom_call_target="tpu_custom_call" | custom-call | flops 3355443200 | bytes 786432 | tf_op jit(solution)/shard_map/inverse_factor/pallas_call | solution.py:102
  127.0 0.9 constant_dynamic-slice_fusion.2
  129.2 5.8 %all-to-all-start.2 = ((f32[32,4,128]{2,1,0:T(4,128)}), f32[32,4,128]{2,1,0:T(4,128)S(1)}, u32[]{:S(2)}, u32[]{:S(2)}) async-start(f32[32,4,128]{2,1,0:T(4,128)} %copy.15), calls=%async_computation.2 | async-start | bytes 131072 | tf_op jit(solution)/shard_map/all_to_all | solution.py:160
  135.1 2.4 %convolution_multiply_fusion = f32[512,256]{1,0:T(8,128)} fusion(f32[256,256]{1,0:T(8,128)} %get-tuple-element.4, f32[256,256]{1,0:T(8,128)S(1)} %add.55, f32[256,256]{1,0:T(8,128)S(1)} %add.53), kind=kOutput, calls=%fused_computation.4 | convolution fusion | flops 402915328 | bytes 1310720 | tf_op jit(solution)/shard_map/dot_general | solution.py:154
  137.4 7.6 %all-to-all-done.2 = f32[32,4,128]{2,1,0:T(4,128)S(1)} async-done(((f32[32,4,128]{2,1,0:T(4,128)}), f32[32,4,128]{2,1,0:T(4,128)S(1)}, u32[]{:S(2)}, u32[]{:S(2)}) %all-to-all-start.2) | async-done | bytes 65568 | tf_op jit(solution)/shard_map/all_to_all | solution.py:160
  (43 shorter events, 7.4 us)
Async XLA Ops:
  8.1 8.1 %collective-permute-start = (f32[256,256]{1,0:T(8,128)S(1)}, f32[256,256]{1,0:T(8,128)S(1)}, u32[]{:S(2)}, u32[]{:S(2)}) collective-permute-start(f32[256,256]{1,0:T(8,128)S(1)} %get-tuple-element.10), channel_id=1, source_target_pairs={{0,1},{1,0},{2,3},{3,2},{4,5},{5,4},{6,7},{7,6},{8,9},{9,8},{10,11... | collective-permute-start | bytes 786440 | tf_op jit(solution)/shard_map/ppermute | solution.py:21
  10.4 6.7 %collective-permute-start.2 = (f32[256,256]{1,0:T(8,128)S(1)}, f32[256,256]{1,0:T(8,128)S(1)}, u32[]{:S(2)}, u32[]{:S(2)}) collective-permute-start(f32[256,256]{1,0:T(8,128)S(1)} %get-tuple-element.11), channel_id=1, source_target_pairs={{0,3},{1,2},{2,1},{3,0},{4,7},{5,6},{6,5},{7,4},{8,11},{9,10},{10,... | collective-permute-start | bytes 786440 | tf_op jit(solution)/shard_map/ppermute | solution.py:21
  17.2 7.0 %collective-permute-start.1 = (f32[256,256]{1,0:T(8,128)S(1)}, f32[256,256]{1,0:T(8,128)S(1)}, u32[]{:S(2)}, u32[]{:S(2)}) collective-permute-start(f32[256,256]{1,0:T(8,128)S(1)} %get-tuple-element.8), channel_id=1, source_target_pairs={{0,3},{1,2},{2,1},{3,0},{4,7},{5,6},{6,5},{7,4},{8,11},{9,10},{10,... | collective-permute-start | bytes 786440 | tf_op jit(solution)/shard_map/ppermute | solution.py:21
  19.0 7.4 %collective-permute-start.3 = (f32[256,256]{1,0:T(8,128)S(1)}, f32[256,256]{1,0:T(8,128)S(1)}, u32[]{:S(2)}, u32[]{:S(2)}) collective-permute-start(f32[256,256]{1,0:T(8,128)S(1)} %get-tuple-element.9), channel_id=1, source_target_pairs={{0,1},{1,0},{2,3},{3,2},{4,5},{5,4},{6,7},{7,6},{8,9},{9,8},{10,11... | collective-permute-start | bytes 786440 | tf_op jit(solution)/shard_map/ppermute | solution.py:21
  34.1 4.2 %collective-permute-start.15 = (f32[4,8,128,128]{3,1,2,0:T(8,128)S(1)}, f32[4,8,128,128]{3,1,2,0:T(8,128)S(1)}, u32[]{:S(2)}, u32[]{:S(2)}) collective-permute-start(f32[4,8,128,128]{3,1,2,0:T(8,128)S(1)} %bitcast.30), channel_id=1, source_target_pairs={{0,4},{4,0},{1,5},{5,1},{2,6},{6,2},{3,7},{7,3},{8,12},{12,8},{9,1... | collective-permute-start | bytes 6291464 | tf_op jit(solution)/shard_map/ppermute | solution.py:21
  40.0 32.1 %all-to-all-start = ((f32[4,8,128,128]{3,1,2,0:T(8,128)}), f32[4,8,128,128]{3,1,2,0:T(8,128)S(1)}, u32[]{:S(2)}, u32[]{:S(2)}) async-start(f32[4,8,128,128]{3,1,2,0:T(8,128)} %fusion), calls=%async_computation | async-start | bytes 4194304 | tf_op jit(solution)/shard_map/all_to_all | solution.py:148
  45.3 1.3 collective-permute-start.4
  46.7 34.9 %collective-permute-start.5 = (f32[64,256]{1,0:T(8,128)S(1)}, f32[64,256]{1,0:T(8,128)S(1)}, u32[]{:S(2)}, u32[]{:S(2)}) collective-permute-start(f32[64,256]{1,0:T(8,128)S(1)} %fusion.14), channel_id=1, source_target_pairs={{0,64},{64,0},{128,192},{192,128},{1,65},{65,1},{129,193},{193,129... | collective-permute-start | bytes 196616 | tf_op jit(solution)/shard_map/ppermute | solution.py:21
  48.8 32.8 %collective-permute-start.6 = (f32[64,256]{1,0:T(8,128)S(1)}, f32[64,256]{1,0:T(8,128)S(1)}, u32[]{:S(2)}, u32[]{:S(2)}) collective-permute-start(f32[64,256]{1,0:T(8,128)S(1)} %fusion.14), channel_id=1, source_target_pairs={{0,128},{64,192},{128,0},{192,64},{1,129},{65,193},{129,1},{193,65... | collective-permute-start | bytes 196616 | tf_op jit(solution)/shard_map/ppermute | solution.py:21
  51.5 30.1 %collective-permute-start.7 = (f32[64,256]{1,0:T(8,128)S(1)}, f32[64,256]{1,0:T(8,128)S(1)}, u32[]{:S(2)}, u32[]{:S(2)}) collective-permute-start(f32[64,256]{1,0:T(8,128)S(1)} %fusion.14), channel_id=1, source_target_pairs={{0,192},{64,128},{128,64},{192,0},{1,193},{65,129},{129,65},{193,1... | collective-permute-start | bytes 196616 | tf_op jit(solution)/shard_map/ppermute | solution.py:21
  73.1 53.7 %all-to-all-start.1 = ((f32[8,128,128]{2,1,0:T(8,128)}), f32[8,128,128]{2,1,0:T(8,128)S(1)}, u32[]{:S(2)}, u32[]{:S(2)}) async-start(f32[8,128,128]{2,1,0:T(8,128)} %copy.13), calls=%async_computation.1 | async-start | bytes 1048576 | tf_op jit(solution)/shard_map/all_to_all | solution.py:149
  81.6 15.6 %collective-permute-start.10 = (f32[64,256]{1,0:T(8,128)S(1)}, f32[64,256]{1,0:T(8,128)S(1)}, u32[]{:S(2)}, u32[]{:S(2)}) collective-permute-start(f32[64,256]{1,0:T(8,128)S(1)} %add_add_fusion.1), channel_id=1, source_target_pairs={{0,24},{8,16},{16,8},{24,0},{32,56},{40,48},{48,40},{56,32},{1,25}... | collective-permute-start | bytes 196616 | tf_op jit(solution)/shard_map/ppermute | solution.py:21
  85.5 11.8 %collective-permute-start.8 = (f32[64,256]{1,0:T(8,128)S(1)}, f32[64,256]{1,0:T(8,128)S(1)}, u32[]{:S(2)}, u32[]{:S(2)}) collective-permute-start(f32[64,256]{1,0:T(8,128)S(1)} %add_add_fusion.1), channel_id=1, source_target_pairs={{0,8},{8,0},{16,24},{24,16},{32,40},{40,32},{48,56},{56,48},{1,9},... | collective-permute-start | bytes 196616 | tf_op jit(solution)/shard_map/ppermute | solution.py:21
  85.6 14.2 %collective-permute-start.9 = (f32[64,256]{1,0:T(8,128)S(1)}, f32[64,256]{1,0:T(8,128)S(1)}, u32[]{:S(2)}, u32[]{:S(2)}) collective-permute-start(f32[64,256]{1,0:T(8,128)S(1)} %add_add_fusion.1), channel_id=1, source_target_pairs={{0,16},{8,24},{16,0},{24,8},{32,48},{40,56},{48,32},{56,40},{1,17}... | collective-permute-start | bytes 196616 | tf_op jit(solution)/shard_map/ppermute | solution.py:21
  99.8 6.3 %collective-permute-start.11 = (f32[64,256]{1,0:T(8,128)S(1)}, f32[64,256]{1,0:T(8,128)S(1)}, u32[]{:S(2)}, u32[]{:S(2)}) collective-permute-start(f32[64,256]{1,0:T(8,128)S(1)} %add_add_fusion), channel_id=1, source_target_pairs={{0,56},{8,48},{16,40},{24,32},{32,24},{40,16},{48,8},{56,0},{1,57}... | collective-permute-start | bytes 196616 | tf_op jit(solution)/shard_map/ppermute | solution.py:21
  106.1 7.6 %copy-start = (f32[64,256]{1,0:T(8,128)}, f32[64,256]{1,0:T(8,128)S(1)}, u32[]{:S(2)}) copy-start(f32[64,256]{1,0:T(8,128)S(1)} %add.64.refs_0_) | copy-start | bytes 196612
  106.1 4.4 %collective-permute-start.12 = (f32[64,256]{1,0:T(8,128)S(1)}, f32[64,256]{1,0:T(8,128)S(1)}, u32[]{:S(2)}, u32[]{:S(2)}) collective-permute-start(f32[64,256]{1,0:T(8,128)S(1)} %add.64.refs_0_), channel_id=1, source_target_pairs={{0,1},{1,0},{2,3},{3,2},{4,5},{5,4},{6,7},{7,6},{8,9},{9,8},{10,11... | collective-permute-start | bytes 196616 | tf_op jit(solution)/shard_map/ppermute | solution.py:21
  107.9 5.8 %collective-permute-start.13 = (f32[64,256]{1,0:T(8,128)S(1)}, f32[64,256]{1,0:T(8,128)S(1)}, u32[]{:S(2)}, u32[]{:S(2)}) collective-permute-start(f32[64,256]{1,0:T(8,128)S(1)} %add.64.refs_0_), channel_id=1, source_target_pairs={{0,2},{1,3},{2,0},{3,1},{4,6},{5,7},{6,4},{7,5},{8,10},{9,11},{10,... | collective-permute-start | bytes 196616 | tf_op jit(solution)/shard_map/ppermute | solution.py:21
  108.4 5.3 %collective-permute-start.14 = (f32[64,256]{1,0:T(8,128)S(1)}, f32[64,256]{1,0:T(8,128)S(1)}, u32[]{:S(2)}, u32[]{:S(2)}) collective-permute-start(f32[64,256]{1,0:T(8,128)S(1)} %add.64.refs_0_), channel_id=1, source_target_pairs={{0,3},{1,2},{2,1},{3,0},{4,7},{5,6},{6,5},{7,4},{8,11},{9,10},{10,... | collective-permute-start | bytes 196616 | tf_op jit(solution)/shard_map/ppermute | solution.py:21
  110.4 3.3 %copy-start.1 = (f32[64,256]{1,0:T(8,128)}, f32[64,256]{1,0:T(8,128)S(1)}, u32[]{:S(2)}) copy-start(f32[64,256]{1,0:T(8,128)S(1)} %collective-permute-done.12.refs_1_) | copy-start | bytes 196612
  113.7 0.6 copy-start.2
  113.7 0.7 copy-start.3
  126.9 1.3 collective-permute-start.16
  129.2 15.8 %all-to-all-start.2 = ((f32[32,4,128]{2,1,0:T(4,128)}), f32[32,4,128]{2,1,0:T(4,128)S(1)}, u32[]{:S(2)}, u32[]{:S(2)}) async-start(f32[32,4,128]{2,1,0:T(4,128)} %copy.15), calls=%async_computation.2 | async-start | bytes 131072 | tf_op jit(solution)/shard_map/all_to_all | solution.py:160

commit v2 on v1

--- a/solution.py
+++ b/solution.py
@@ -1,5 +1,3 @@
-import functools
-
 import jax
 import jax.numpy as jnp
 from jax import lax
@@ -97,7 +95,7 @@
 
 
 def inverse_factor(parts, place):
-    rows, size = parts[0].shape
+    _, size = parts[0].shape
     vmem = pl.BlockSpec(memory_space=pltpu.VMEM)
     return pl.pallas_call(
         factor_kernel,
@@ -109,27 +107,30 @@
         out_specs=(vmem, vmem),
         scratch_shapes=[pltpu.VMEM((size, size), jnp.float32)],
         cost_estimate=pl.CostEstimate(flops=4 * size**3 * 50, bytes_accessed=12 * size * size, transcendentals=size),
+        compiler_params=pltpu.CompilerParams(vmem_limit_bytes=12 << 20),
         name="inverse_factor",
     )(place, *parts)
 
 
 def group_sum(value, axis):
-    one, two, three = (swap(value, axis, k) for k in (1, 2, 3))
+    one, three, two = (swap(value, axis, k) for k in (1, 3, 2))
     return (value + one) + (two + three)
 
 
-def shards(jacobian, probe):
+def compute(jacobian, probe):
     width = probe.shape[1]
     columns = jacobian.shape[1]
     nx, nz, nc, ns = (lax.axis_size(a) for a in ("x", "z", "core", "slab"))
     total_rows = jacobian.shape[0] * nx * nz * nc
     slab, core = lax.axis_index("slab"), lax.axis_index("core")
 
+    middle = jacobian.shape[0] // 2
     partial_value = jnp.dot(jacobian, probe, precision=HIGH, preferred_element_type=jnp.float32)
-    middle = jacobian.shape[0] // 2
     top, bottom = partial_value[:middle], partial_value[middle:]
-    top, bottom = top + swap(top, "slab", 1), bottom + swap(bottom, "slab", 3)
-    top, bottom = top + swap(top, "slab", 3), bottom + swap(bottom, "slab", 1)
+    top = top + swap(top, "slab", 1)
+    bottom = bottom + swap(bottom, "slab", 3)
+    top = top + swap(top, "slab", 3)
+    bottom = bottom + swap(bottom, "slab", 1)
     sketch = jnp.concatenate([top, bottom], axis=0)
 
     gram = jnp.dot(sketch.T, sketch, precision=HIGHEST, preferred_element_type=jnp.float32)
@@ -165,7 +166,7 @@
     grid = Mesh(mesh.devices.reshape(4, 8, 2, 4), ("x", "z", "core", "slab"))
     site = ("x", "z", "core")
     return jax.shard_map(
-        shards,
+        compute,
         mesh=grid,
         in_specs=(P(site, "slab"), P("slab", None)),
         out_specs=(P(site, None), P(site, "slab")),

time: 148 us -> 146 us (0.986)
  waiting for transfers between devices: 65.7 us -> 67.6 us
  Pallas kernels: 12.5 us -> 10.8 us
  local copies, waits for them, and re-layouts: 5.25 us -> 3.7 us
    pallas_call x1, Pallas kernels: 12.5 us -> 10.8 us  [inverse_factor(): pl.pallas_call(factor_kernel, out_shape=(jax.ShapeDtypeStruct((size, size...]
  transfers between devices with their start and end apart: 20 -> 20, of which waited for: 14 -> 14; matrix products, arithmetic and copies ran while one was open for 4% -> 3% of each run, Pallas kernels for 9% -> 8%
where the time goes in v2:
time: 146 us; the launch traced here: 143 us
  waiting for transfers between devices  67.6 us (46%)
  starting transfers between devices  42 us (29%)
  matrix products  16.3 us (11%)
  Pallas kernels  10.8 us (7%)
  local copies, waits for them, and re-layouts  3.7 us (3%)
  other arithmetic  2.04 us (1%)
    ppermute x17, waiting for transfers between devices, swap(): return lax.ppermute(value, axis, pairs(lax.axis_size(axis), mask))  38.5 us
    ppermute x17, starting transfers between devices, swap(): return lax.ppermute(value, axis, pairs(lax.axis_size(axis), mask))  23.5 us
    all_to_all x1, waiting for transfers between devices, compute(): mine = lax.all_to_all(mine, 'x', 0, 0).sum(0)  20.5 us
    pallas_call x1, Pallas kernels, inverse_factor(): pl.pallas_call(factor_kernel, out_shape=(jax.ShapeDtypeStruct((size, size...  10.8 us
    all_to_all x1, waiting for transfers between devices, compute(): owned = lax.all_to_all(owned, ('x', 'z'), 0, 0)  8.59 us
    all_to_all x1, starting transfers between devices, compute(): mine = lax.all_to_all(mine, 'z', 0, 0).sum(0)  8.46 us
    dot_general x1, matrix products, compute(): jnp.dot(jacobian, probe, precision=HIGH, preferred_element_type=jnp.float32)  7.46 us
    dot_general x1, matrix products, compute(): jnp.dot(sketch.T, jacobian, precision=HIGH, preferred_element_type=jnp.fl...  6.19 us
  transfers between devices with their start and end apart: 20, of which 14 were waited for; matrix products, arithmetic and copies ran while one was open for 3% of the time, Pallas kernels for 8%

profile of v2, /device:TPU:8, one launch (start us, length us, event | category | flops | bytes accessed | tf_op | source)
XLA Modules:
  0.0 143.3 jit_solution(3294633858333281239)
XLA Ops:
  0.6 7.5 %fusion.8 = f32[512,256]{1,0:T(8,128)S(1)} fusion(f32[512,4096]{1,0:T(8,128)} %param.2, f32[4096,256]{1,0:T(8,128)} %param.3), kind=kOutput, calls=%fused_computation.22 | convolution fusion | flops 3221225472 | bytes 13107200 | tf_op jit(solution)/shard_map/dot_general | solution.py:128
  8.1 2.2 %collective-permute-start = (f32[256,256]{1,0:T(8,128)S(1)}, f32[256,256]{1,0:T(8,128)S(1)}, u32[]{:S(2)}, u32[]{:S(2)}) collective-permute-start(f32[256,256]{1,0:T(8,128)S(1)} %get-tuple-element.10), channel_id=1, source_target_pairs={{0,1},{1,0},{2,3},{3,2},{4,5},{5,4},{6,7},{7,6},{8,9},{9,8},{10,11... | collective-permute-start | bytes 786440 | tf_op jit(solution)/shard_map/ppermute | solution.py:19
  11.1 5.2 %collective-permute-done = f32[256,256]{1,0:T(8,128)S(1)} collective-permute-done((f32[256,256]{1,0:T(8,128)S(1)}, f32[256,256]{1,0:T(8,128)S(1)}, u32[]{:S(2)}, u32[]{:S(2)}) %collective-permute-start) | collective-permute-done | bytes 262176 | tf_op jit(solution)/shard_map/ppermute | solution.py:19
  16.3 0.8 collective-permute-done.2
  17.2 1.8 %collective-permute-start.1 = (f32[256,256]{1,0:T(8,128)S(1)}, f32[256,256]{1,0:T(8,128)S(1)}, u32[]{:S(2)}, u32[]{:S(2)}) collective-permute-start(f32[256,256]{1,0:T(8,128)S(1)} %get-tuple-element.8), channel_id=1, source_target_pairs={{0,3},{1,2},{2,1},{3,0},{4,7},{5,6},{6,5},{7,4},{8,11},{9,10},{10,... | collective-permute-start | bytes 786440 | tf_op jit(solution)/shard_map/ppermute | solution.py:19
  19.0 2.6 %collective-permute-start.3 = (f32[256,256]{1,0:T(8,128)S(1)}, f32[256,256]{1,0:T(8,128)S(1)}, u32[]{:S(2)}, u32[]{:S(2)}) collective-permute-start(f32[256,256]{1,0:T(8,128)S(1)} %get-tuple-element.9), channel_id=1, source_target_pairs={{0,1},{1,0},{2,3},{3,2},{4,5},{5,4},{6,7},{7,6},{8,9},{9,8},{10,11... | collective-permute-start | bytes 786440 | tf_op jit(solution)/shard_map/ppermute | solution.py:19
  21.6 2.6 %collective-permute-done.1 = f32[256,256]{1,0:T(8,128)S(1)} collective-permute-done((f32[256,256]{1,0:T(8,128)S(1)}, f32[256,256]{1,0:T(8,128)S(1)}, u32[]{:S(2)}, u32[]{:S(2)}) %collective-permute-start.1) | collective-permute-done | bytes 262176 | tf_op jit(solution)/shard_map/ppermute | solution.py:19
  24.2 2.2 %collective-permute-done.3 = f32[256,256]{1,0:T(8,128)S(1)} collective-permute-done((f32[256,256]{1,0:T(8,128)S(1)}, f32[256,256]{1,0:T(8,128)S(1)}, u32[]{:S(2)}, u32[]{:S(2)}) %collective-permute-start.3) | collective-permute-done | bytes 262176 | tf_op jit(solution)/shard_map/ppermute | solution.py:19
  26.5 6.2 %convolution_bitcast_fusion = f32[32,8,32,128]{3,1,2,0:T(8,128)S(1)} fusion(f32[512,4096]{1,0:T(8,128)} %param.2, f32[256,256]{1,0:T(8,128)S(1)} %add.55, f32[256,256]{1,0:T(8,128)S(1)} %add.53), kind=kOutput, calls=%fused_computation | convolution fusion | flops 3221356544 | bytes 13107200 | tf_op jit(solution)/shard_map/dot_general | solution.py:144
  34.2 4.1 %collective-permute-done.15 = f32[4,8,128,128]{3,1,2,0:T(8,128)S(1)} collective-permute-done((f32[4,8,128,128]{3,1,2,0:T(8,128)S(1)}, f32[4,8,128,128]{3,1,2,0:T(8,128)S(1)}, u32[]{:S(2)}, u32[]{:S(2)}) %collective-permute-start.15) | collective-permute-done | bytes 2097184 | tf_op jit(solution)/shard_map/ppermute | solution.py:19
  38.3 1.7 %fusion = f32[4,8,128,128]{3,1,2,0:T(8,128)} fusion(f32[4,8,128,128]{3,1,2,0:T(8,128)S(1)} %collective-permute-done.15, f32[1,128,4,8,128]{4,3,2,1,0:T(8,128)S(1)} %get-tuple-element.6), kind=kLoop, calls=%fused_computation.3 | loop fusion | flops 524288 | bytes 6291456 | tf_op jit(solution)/shard_map/add | solution.py:148
  40.0 4.3 %all-to-all-start = ((f32[4,8,128,128]{3,1,2,0:T(8,128)}), f32[4,8,128,128]{3,1,2,0:T(8,128)S(1)}, u32[]{:S(2)}, u32[]{:S(2)}) async-start(f32[4,8,128,128]{3,1,2,0:T(8,128)} %fusion), calls=%async_computation | async-start | bytes 4194304 | tf_op jit(solution)/shard_map/all_to_all | solution.py:149
  44.3 1.0 fusion.1
  45.4 1.2 collective-permute-done.4
  46.7 2.1 %collective-permute-start.5 = (f32[64,256]{1,0:T(8,128)S(1)}, f32[64,256]{1,0:T(8,128)S(1)}, u32[]{:S(2)}, u32[]{:S(2)}) collective-permute-start(f32[64,256]{1,0:T(8,128)S(1)} %fusion.14), channel_id=1, source_target_pairs={{0,64},{64,0},{128,192},{192,128},{1,65},{65,1},{129,193},{193,129... | collective-permute-start | bytes 196616 | tf_op jit(solution)/shard_map/ppermute | solution.py:19
  48.8 2.7 %collective-permute-start.6 = (f32[64,256]{1,0:T(8,128)S(1)}, f32[64,256]{1,0:T(8,128)S(1)}, u32[]{:S(2)}, u32[]{:S(2)}) collective-permute-start(f32[64,256]{1,0:T(8,128)S(1)} %fusion.14), channel_id=1, source_target_pairs={{0,128},{64,192},{128,0},{192,64},{1,129},{65,193},{129,1},{193,65... | collective-permute-start | bytes 196616 | tf_op jit(solution)/shard_map/ppermute | solution.py:19
  51.6 20.5 %all-to-all-done = f32[4,8,128,128]{3,1,2,0:T(8,128)S(1)} async-done(((f32[4,8,128,128]{3,1,2,0:T(8,128)}), f32[4,8,128,128]{3,1,2,0:T(8,128)S(1)}, u32[]{:S(2)}, u32[]{:S(2)}) %all-to-all-start) | async-done | bytes 2097184 | tf_op jit(solution)/shard_map/all_to_all | solution.py:149
  72.2 0.9 copy.13
  73.1 8.5 %all-to-all-start.1 = ((f32[8,128,128]{2,1,0:T(8,128)}), f32[8,128,128]{2,1,0:T(8,128)S(1)}, u32[]{:S(2)}, u32[]{:S(2)}) async-start(f32[8,128,128]{2,1,0:T(8,128)} %copy.13), calls=%async_computation.1 | async-start | bytes 1048576 | tf_op jit(solution)/shard_map/all_to_all | solution.py:150
  81.6 3.9 %collective-permute-start.10 = (f32[64,256]{1,0:T(8,128)S(1)}, f32[64,256]{1,0:T(8,128)S(1)}, u32[]{:S(2)}, u32[]{:S(2)}) collective-permute-start(f32[64,256]{1,0:T(8,128)S(1)} %add_add_fusion.1), channel_id=1, source_target_pairs={{0,24},{8,16},{16,8},{24,0},{32,56},{40,48},{48,40},{56,32},{1,25}... | collective-permute-start | bytes 196616 | tf_op jit(solution)/shard_map/ppermute | solution.py:19
  86.2 11.1 %collective-permute-done.10 = f32[64,256]{1,0:T(8,128)S(1)} collective-permute-done((f32[64,256]{1,0:T(8,128)S(1)}, f32[64,256]{1,0:T(8,128)S(1)}, u32[]{:S(2)}, u32[]{:S(2)}) %collective-permute-start.10) | collective-permute-done | bytes 65568 | tf_op jit(solution)/shard_map/ppermute | solution.py:19
  97.3 2.5 %collective-permute-done.9 = f32[64,256]{1,0:T(8,128)S(1)} collective-permute-done((f32[64,256]{1,0:T(8,128)S(1)}, f32[64,256]{1,0:T(8,128)S(1)}, u32[]{:S(2)}, u32[]{:S(2)}) %collective-permute-start.9) | collective-permute-done | bytes 65568 | tf_op jit(solution)/shard_map/ppermute | solution.py:19
  99.8 2.8 %collective-permute-start.11 = (f32[64,256]{1,0:T(8,128)S(1)}, f32[64,256]{1,0:T(8,128)S(1)}, u32[]{:S(2)}, u32[]{:S(2)}) collective-permute-start(f32[64,256]{1,0:T(8,128)S(1)} %add_add_fusion), channel_id=1, source_target_pairs={{0,56},{8,48},{16,40},{24,32},{32,24},{40,16},{48,8},{56,0},{1,57}... | collective-permute-start | bytes 196616 | tf_op jit(solution)/shard_map/ppermute | solution.py:19
  102.6 3.4 %collective-permute-done.11 = f32[64,256]{1,0:T(8,128)S(1)} collective-permute-done((f32[64,256]{1,0:T(8,128)S(1)}, f32[64,256]{1,0:T(8,128)S(1)}, u32[]{:S(2)}, u32[]{:S(2)}) %collective-permute-start.11) | collective-permute-done | bytes 65568 | tf_op jit(solution)/shard_map/ppermute | solution.py:19
  106.1 1.8 %collective-permute-start.12 = (f32[64,256]{1,0:T(8,128)S(1)}, f32[64,256]{1,0:T(8,128)S(1)}, u32[]{:S(2)}, u32[]{:S(2)}) collective-permute-start(f32[64,256]{1,0:T(8,128)S(1)} %add.64.refs_0_), channel_id=1, source_target_pairs={{0,1},{1,0},{2,3},{3,2},{4,5},{5,4},{6,7},{7,6},{8,9},{9,8},{10,11... | collective-permute-start | bytes 196616 | tf_op jit(solution)/shard_map/ppermute | solution.py:19
  108.4 1.3 collective-permute-start.14
  110.4 3.2 %collective-permute-done.13.refs_2_ = f32[64,256]{1,0:T(8,128)S(1)} collective-permute-done((f32[64,256]{1,0:T(8,128)S(1)}, f32[64,256]{1,0:T(8,128)S(1)}, u32[]{:S(2)}, u32[]{:S(2)}) %collective-permute-start.13) | collective-permute-done | bytes 65568 | tf_op jit(solution)/shard_map/ppermute | solution.py:19
  113.7 10.8 %inverse_factor.1 = (f32[256,256]{1,0:T(8,128)S(1)}, f32[2,128,256]{2,1,0:T(8,128)S(1)}) custom-call(s32[1]{0:T(128)} %bitcast.place_ref, f32[64,256]{1,0:T(8,128)S(1)} %add.64.refs_0_, f32[64,256]{1,0:T(8,128)S(1)} %collective-permute-done.12.refs_1_, f32[64,256]{1,0:T(8,128)S(1)} %collective-permute-done.13.refs_2_, ...), custom_call_target="tpu_custom_call" | custom-call | flops 3355443200 | bytes 786432 | tf_op jit(solution)/shard_map/inverse_factor/pallas_call | solution.py:100
  124.7 1.2 collective-permute-done.16
  126.8 5.8 %all-to-all-start.2 = ((f32[32,4,128]{2,1,0:T(4,128)}), f32[32,4,128]{2,1,0:T(4,128)S(1)}, u32[]{:S(2)}, u32[]{:S(2)}) async-start(f32[32,4,128]{2,1,0:T(4,128)} %copy.15), calls=%async_computation.2 | async-start | bytes 131072 | tf_op jit(solution)/shard_map/all_to_all | solution.py:161
  132.7 1.4 convolution_multiply_fusion
  134.1 8.6 %all-to-all-done.2 = f32[32,4,128]{2,1,0:T(4,128)S(1)} async-done(((f32[32,4,128]{2,1,0:T(4,128)}), f32[32,4,128]{2,1,0:T(4,128)S(1)}, u32[]{:S(2)}, u32[]{:S(2)}) %all-to-all-start.2) | async-done | bytes 65568 | tf_op jit(solution)/shard_map/all_to_all | solution.py:161
  (35 shorter events, 6.5 us)
Async XLA Ops:
  8.1 8.1 %collective-permute-start = (f32[256,256]{1,0:T(8,128)S(1)}, f32[256,256]{1,0:T(8,128)S(1)}, u32[]{:S(2)}, u32[]{:S(2)}) collective-permute-start(f32[256,256]{1,0:T(8,128)S(1)} %get-tuple-element.10), channel_id=1, source_target_pairs={{0,1},{1,0},{2,3},{3,2},{4,5},{5,4},{6,7},{7,6},{8,9},{9,8},{10,11... | collective-permute-start | bytes 786440 | tf_op jit(solution)/shard_map/ppermute | solution.py:19
  10.4 6.7 %collective-permute-start.2 = (f32[256,256]{1,0:T(8,128)S(1)}, f32[256,256]{1,0:T(8,128)S(1)}, u32[]{:S(2)}, u32[]{:S(2)}) collective-permute-start(f32[256,256]{1,0:T(8,128)S(1)} %get-tuple-element.11), channel_id=1, source_target_pairs={{0,3},{1,2},{2,1},{3,0},{4,7},{5,6},{6,5},{7,4},{8,11},{9,10},{10,... | collective-permute-start | bytes 786440 | tf_op jit(solution)/shard_map/ppermute | solution.py:19
  17.2 7.0 %collective-permute-start.1 = (f32[256,256]{1,0:T(8,128)S(1)}, f32[256,256]{1,0:T(8,128)S(1)}, u32[]{:S(2)}, u32[]{:S(2)}) collective-permute-start(f32[256,256]{1,0:T(8,128)S(1)} %get-tuple-element.8), channel_id=1, source_target_pairs={{0,3},{1,2},{2,1},{3,0},{4,7},{5,6},{6,5},{7,4},{8,11},{9,10},{10,... | collective-permute-start | bytes 786440 | tf_op jit(solution)/shard_map/ppermute | solution.py:19
  19.0 7.4 %collective-permute-start.3 = (f32[256,256]{1,0:T(8,128)S(1)}, f32[256,256]{1,0:T(8,128)S(1)}, u32[]{:S(2)}, u32[]{:S(2)}) collective-permute-start(f32[256,256]{1,0:T(8,128)S(1)} %get-tuple-element.9), channel_id=1, source_target_pairs={{0,1},{1,0},{2,3},{3,2},{4,5},{5,4},{6,7},{7,6},{8,9},{9,8},{10,11... | collective-permute-start | bytes 786440 | tf_op jit(solution)/shard_map/ppermute | solution.py:19
  34.1 4.2 %collective-permute-start.15 = (f32[4,8,128,128]{3,1,2,0:T(8,128)S(1)}, f32[4,8,128,128]{3,1,2,0:T(8,128)S(1)}, u32[]{:S(2)}, u32[]{:S(2)}) collective-permute-start(f32[4,8,128,128]{3,1,2,0:T(8,128)S(1)} %bitcast.30), channel_id=1, source_target_pairs={{0,4},{4,0},{1,5},{5,1},{2,6},{6,2},{3,7},{7,3},{8,12},{12,8},{9,1... | collective-permute-start | bytes 6291464 | tf_op jit(solution)/shard_map/ppermute | solution.py:19
  40.0 32.1 %all-to-all-start = ((f32[4,8,128,128]{3,1,2,0:T(8,128)}), f32[4,8,128,128]{3,1,2,0:T(8,128)S(1)}, u32[]{:S(2)}, u32[]{:S(2)}) async-start(f32[4,8,128,128]{3,1,2,0:T(8,128)} %fusion), calls=%async_computation | async-start | bytes 4194304 | tf_op jit(solution)/shard_map/all_to_all | solution.py:149
  45.3 1.3 collective-permute-start.4
  46.7 34.9 %collective-permute-start.5 = (f32[64,256]{1,0:T(8,128)S(1)}, f32[64,256]{1,0:T(8,128)S(1)}, u32[]{:S(2)}, u32[]{:S(2)}) collective-permute-start(f32[64,256]{1,0:T(8,128)S(1)} %fusion.14), channel_id=1, source_target_pairs={{0,64},{64,0},{128,192},{192,128},{1,65},{65,1},{129,193},{193,129... | collective-permute-start | bytes 196616 | tf_op jit(solution)/shard_map/ppermute | solution.py:19
  48.8 32.8 %collective-permute-start.6 = (f32[64,256]{1,0:T(8,128)S(1)}, f32[64,256]{1,0:T(8,128)S(1)}, u32[]{:S(2)}, u32[]{:S(2)}) collective-permute-start(f32[64,256]{1,0:T(8,128)S(1)} %fusion.14), channel_id=1, source_target_pairs={{0,128},{64,192},{128,0},{192,64},{1,129},{65,193},{129,1},{193,65... | collective-permute-start | bytes 196616 | tf_op jit(solution)/shard_map/ppermute | solution.py:19
  51.5 30.1 %collective-permute-start.7 = (f32[64,256]{1,0:T(8,128)S(1)}, f32[64,256]{1,0:T(8,128)S(1)}, u32[]{:S(2)}, u32[]{:S(2)}) collective-permute-start(f32[64,256]{1,0:T(8,128)S(1)} %fusion.14), channel_id=1, source_target_pairs={{0,192},{64,128},{128,64},{192,0},{1,193},{65,129},{129,65},{193,1... | collective-permute-start | bytes 196616 | tf_op jit(solution)/shard_map/ppermute | solution.py:19
  73.1 51.3 %all-to-all-start.1 = ((f32[8,128,128]{2,1,0:T(8,128)}), f32[8,128,128]{2,1,0:T(8,128)S(1)}, u32[]{:S(2)}, u32[]{:S(2)}) async-start(f32[8,128,128]{2,1,0:T(8,128)} %copy.13), calls=%async_computation.1 | async-start | bytes 1048576 | tf_op jit(solution)/shard_map/all_to_all | solution.py:150
  81.6 15.6 %collective-permute-start.10 = (f32[64,256]{1,0:T(8,128)S(1)}, f32[64,256]{1,0:T(8,128)S(1)}, u32[]{:S(2)}, u32[]{:S(2)}) collective-permute-start(f32[64,256]{1,0:T(8,128)S(1)} %add_add_fusion.1), channel_id=1, source_target_pairs={{0,24},{8,16},{16,8},{24,0},{32,56},{40,48},{48,40},{56,32},{1,25}... | collective-permute-start | bytes 196616 | tf_op jit(solution)/shard_map/ppermute | solution.py:19
  85.5 11.8 %collective-permute-start.8 = (f32[64,256]{1,0:T(8,128)S(1)}, f32[64,256]{1,0:T(8,128)S(1)}, u32[]{:S(2)}, u32[]{:S(2)}) collective-permute-start(f32[64,256]{1,0:T(8,128)S(1)} %add_add_fusion.1), channel_id=1, source_target_pairs={{0,8},{8,0},{16,24},{24,16},{32,40},{40,32},{48,56},{56,48},{1,9},... | collective-permute-start | bytes 196616 | tf_op jit(solution)/shard_map/ppermute | solution.py:19
  85.6 14.2 %collective-permute-start.9 = (f32[64,256]{1,0:T(8,128)S(1)}, f32[64,256]{1,0:T(8,128)S(1)}, u32[]{:S(2)}, u32[]{:S(2)}) collective-permute-start(f32[64,256]{1,0:T(8,128)S(1)} %add_add_fusion.1), channel_id=1, source_target_pairs={{0,16},{8,24},{16,0},{24,8},{32,48},{40,56},{48,32},{56,40},{1,17}... | collective-permute-start | bytes 196616 | tf_op jit(solution)/shard_map/ppermute | solution.py:19
  99.8 6.3 %collective-permute-start.11 = (f32[64,256]{1,0:T(8,128)S(1)}, f32[64,256]{1,0:T(8,128)S(1)}, u32[]{:S(2)}, u32[]{:S(2)}) collective-permute-start(f32[64,256]{1,0:T(8,128)S(1)} %add_add_fusion), channel_id=1, source_target_pairs={{0,56},{8,48},{16,40},{24,32},{32,24},{40,16},{48,8},{56,0},{1,57}... | collective-permute-start | bytes 196616 | tf_op jit(solution)/shard_map/ppermute | solution.py:19
  106.1 4.4 %collective-permute-start.12 = (f32[64,256]{1,0:T(8,128)S(1)}, f32[64,256]{1,0:T(8,128)S(1)}, u32[]{:S(2)}, u32[]{:S(2)}) collective-permute-start(f32[64,256]{1,0:T(8,128)S(1)} %add.64.refs_0_), channel_id=1, source_target_pairs={{0,1},{1,0},{2,3},{3,2},{4,5},{5,4},{6,7},{7,6},{8,9},{9,8},{10,11... | collective-permute-start | bytes 196616 | tf_op jit(solution)/shard_map/ppermute | solution.py:19
  107.9 5.8 %collective-permute-start.13 = (f32[64,256]{1,0:T(8,128)S(1)}, f32[64,256]{1,0:T(8,128)S(1)}, u32[]{:S(2)}, u32[]{:S(2)}) collective-permute-start(f32[64,256]{1,0:T(8,128)S(1)} %add.64.refs_0_), channel_id=1, source_target_pairs={{0,2},{1,3},{2,0},{3,1},{4,6},{5,7},{6,4},{7,5},{8,10},{9,11},{10,... | collective-permute-start | bytes 196616 | tf_op jit(solution)/shard_map/ppermute | solution.py:19
  108.4 5.3 %collective-permute-start.14 = (f32[64,256]{1,0:T(8,128)S(1)}, f32[64,256]{1,0:T(8,128)S(1)}, u32[]{:S(2)}, u32[]{:S(2)}) collective-permute-start(f32[64,256]{1,0:T(8,128)S(1)} %add.64.refs_0_), channel_id=1, source_target_pairs={{0,3},{1,2},{2,1},{3,0},{4,7},{5,6},{6,5},{7,4},{8,11},{9,10},{10,... | collective-permute-start | bytes 196616 | tf_op jit(solution)/shard_map/ppermute | solution.py:19
  124.5 1.3 collective-permute-start.16
  126.8 15.8 %all-to-all-start.2 = ((f32[32,4,128]{2,1,0:T(4,128)}), f32[32,4,128]{2,1,0:T(4,128)S(1)}, u32[]{:S(2)}, u32[]{:S(2)}) async-start(f32[32,4,128]{2,1,0:T(4,128)} %copy.15), calls=%async_computation.2 | async-start | bytes 131072 | tf_op jit(solution)/shard_map/all_to_all | solution.py:161

commit v3 on v2

--- a/solution.py
+++ b/solution.py
@@ -1,3 +1,5 @@
+import functools
+
 import jax
 import jax.numpy as jnp
 from jax import lax
@@ -112,6 +114,33 @@
     )(place, *parts)
 
 
+def owned_kernel(core_ref, split_ref, mine_ref, across_ref, out_ref):
+    core = core_ref[0]
+    rows = split_ref[core]
+    half = mine_ref.shape[0]
+    mine, across = mine_ref[...], across_ref[...]
+    dot = functools.partial(jnp.dot, precision=HIGHEST, preferred_element_type=jnp.float32)
+    upper, lower = jnp.where(core == 0, mine, across), jnp.where(core == 0, across, mine)
+    value = dot(rows[:, :half], upper) + dot(rows[:, half:], lower)
+    step = out_ref.shape[1]
+    for t in range(out_ref.shape[0]):
+        out_ref[t] = value[step * t : step * t + step]
+
+
+def owned_of(split, mine, across, core, sites):
+    vmem = pl.BlockSpec(memory_space=pltpu.VMEM)
+    rows = split.shape[1]
+    return pl.pallas_call(
+        owned_kernel,
+        out_shape=jax.ShapeDtypeStruct((sites, rows // sites, mine.shape[1]), jnp.float32),
+        in_specs=[pl.BlockSpec(memory_space=pltpu.SMEM), vmem, vmem, vmem],
+        out_specs=vmem,
+        compiler_params=pltpu.CompilerParams(vmem_limit_bytes=12 << 20),
+        cost_estimate=pl.CostEstimate(flops=12 * rows * rows * 256, bytes_accessed=1 << 19, transcendentals=0),
+        name="owned_rows",
+    )(core.reshape(1), split, mine, across)
+
+
 def group_sum(value, axis):
     one, three, two = (swap(value, axis, k) for k in (1, 3, 2))
     return (value + one) + (two + three)
@@ -149,15 +178,11 @@
     mine = lax.all_to_all(mine, "x", 0, 0).sum(0)
     mine = lax.all_to_all(mine, "z", 0, 0).sum(0)
     across = swap(mine, "core", 1)
-    terms = jnp.where(core == 0, jnp.stack([mine, across]), jnp.stack([across, mine])).reshape(width, -1)
-
     whole, split = inverse_factor(parts, slab.reshape(1))
     basis = jnp.sqrt(jnp.float32(total_rows)) * lax.dot_general(
         sketch, whole, (((1,), (1,)), ((), ())), precision=HIGHEST, preferred_element_type=jnp.float32
     )
-    rows = lax.dynamic_index_in_dim(split, core, 0, keepdims=False)
-    owned = jnp.dot(rows, terms, precision=HIGHEST, preferred_element_type=jnp.float32)
-    owned = owned.reshape(nx * nz, width // (nx * nz * nc), -1)
+    owned = owned_of(split, mine, across, core, nx * nz)
     owned = lax.all_to_all(owned, ("x", "z"), 0, 0)
     return basis, owned.transpose(1, 0, 2).reshape(owned.shape[1], columns)
 

time: 146 us -> 144 us (0.986)
  waiting for transfers between devices: 67.6 us -> 66.1 us
    ppermute x17, waiting for transfers between devices: 38.5 us -> 32.1 us  [swap(): return lax.ppermute(value, axis, pairs(lax.axis_size(axis), mask))]
    all_to_all x1, waiting for transfers between devices: 20.5 us -> 25.5 us  [compute(): mine = lax.all_to_all(mine, 'x', 0, 0).sum(0)]
  transfers between devices with their start and end apart: 20 -> 20, of which waited for: 14 -> 15; matrix products, arithmetic and copies ran while one was open for 3% -> 3% of each run, Pallas kernels for 8% -> 8%
where the time goes in v3:
time: 144 us; the launch traced here: 142 us
  waiting for transfers between devices  66.1 us (46%)
  starting transfers between devices  42.7 us (30%)
  matrix products  16.1 us (11%)
  Pallas kernels  11.7 us (8%)
  local copies, waits for them, and re-layouts  2.97 us (2%)
  other arithmetic  2.03 us (1%)
    ppermute x17, waiting for transfers between devices, swap(): return lax.ppermute(value, axis, pairs(lax.axis_size(axis), mask))  32.1 us
    all_to_all x1, waiting for transfers between devices, compute(): mine = lax.all_to_all(mine, 'x', 0, 0).sum(0)  25.5 us
    ppermute x17, starting transfers between devices, swap(): return lax.ppermute(value, axis, pairs(lax.axis_size(axis), mask))  23.5 us
    pallas_call x1, Pallas kernels, inverse_factor(): pl.pallas_call(factor_kernel, out_shape=(jax.ShapeDtypeStruct((size, size...  10.8 us
    all_to_all x1, waiting for transfers between devices, compute(): owned = lax.all_to_all(owned, ('x', 'z'), 0, 0)  8.59 us
    all_to_all x1, starting transfers between devices, compute(): mine = lax.all_to_all(mine, 'z', 0, 0).sum(0)  8.46 us
    dot_general x1, matrix products, compute(): jnp.dot(jacobian, probe, precision=HIGH, preferred_element_type=jnp.float32)  7.46 us
    all_to_all x1, starting transfers between devices, compute(): owned = lax.all_to_all(owned, ('x', 'z'), 0, 0)  6.43 us
  transfers between devices with their start and end apart: 20, of which 15 were waited for; matrix products, arithmetic and copies ran while one was open for 3% of the time, Pallas kernels for 8%

profile of v3, /device:TPU:8, one launch (start us, length us, event | category | flops | bytes accessed | tf_op | source)
XLA Modules:
  0.0 142.4 jit_solution(8680661780069481350)
XLA Ops:
  0.6 7.5 %fusion.6 = f32[512,256]{1,0:T(8,128)S(1)} fusion(f32[512,4096]{1,0:T(8,128)} %param.2, f32[4096,256]{1,0:T(8,128)} %param.3), kind=kOutput, calls=%fused_computation.18 | convolution fusion | flops 3221225472 | bytes 13107200 | tf_op jit(solution)/shard_map/dot_general | solution.py:157
  8.1 2.2 %collective-permute-start = (f32[256,256]{1,0:T(8,128)S(1)}, f32[256,256]{1,0:T(8,128)S(1)}, u32[]{:S(2)}, u32[]{:S(2)}) collective-permute-start(f32[256,256]{1,0:T(8,128)S(1)} %get-tuple-element.10), channel_id=1, source_target_pairs={{0,1},{1,0},{2,3},{3,2},{4,5},{5,4},{6,7},{7,6},{8,9},{9,8},{10,11... | collective-permute-start | bytes 786440 | tf_op jit(solution)/shard_map/ppermute | solution.py:21
  11.1 5.2 %collective-permute-done = f32[256,256]{1,0:T(8,128)S(1)} collective-permute-done((f32[256,256]{1,0:T(8,128)S(1)}, f32[256,256]{1,0:T(8,128)S(1)}, u32[]{:S(2)}, u32[]{:S(2)}) %collective-permute-start) | collective-permute-done | bytes 262176 | tf_op jit(solution)/shard_map/ppermute | solution.py:21
  17.2 1.8 %collective-permute-start.1 = (f32[256,256]{1,0:T(8,128)S(1)}, f32[256,256]{1,0:T(8,128)S(1)}, u32[]{:S(2)}, u32[]{:S(2)}) collective-permute-start(f32[256,256]{1,0:T(8,128)S(1)} %get-tuple-element.8), channel_id=1, source_target_pairs={{0,3},{1,2},{2,1},{3,0},{4,7},{5,6},{6,5},{7,4},{8,11},{9,10},{10,... | collective-permute-start | bytes 786440 | tf_op jit(solution)/shard_map/ppermute | solution.py:21
  19.0 2.6 %collective-permute-start.3 = (f32[256,256]{1,0:T(8,128)S(1)}, f32[256,256]{1,0:T(8,128)S(1)}, u32[]{:S(2)}, u32[]{:S(2)}) collective-permute-start(f32[256,256]{1,0:T(8,128)S(1)} %get-tuple-element.9), channel_id=1, source_target_pairs={{0,1},{1,0},{2,3},{3,2},{4,5},{5,4},{6,7},{7,6},{8,9},{9,8},{10,11... | collective-permute-start | bytes 786440 | tf_op jit(solution)/shard_map/ppermute | solution.py:21
  21.6 2.6 %collective-permute-done.1 = f32[256,256]{1,0:T(8,128)S(1)} collective-permute-done((f32[256,256]{1,0:T(8,128)S(1)}, f32[256,256]{1,0:T(8,128)S(1)}, u32[]{:S(2)}, u32[]{:S(2)}) %collective-permute-start.1) | collective-permute-done | bytes 262176 | tf_op jit(solution)/shard_map/ppermute | solution.py:21
  24.2 2.2 %collective-permute-done.3 = f32[256,256]{1,0:T(8,128)S(1)} collective-permute-done((f32[256,256]{1,0:T(8,128)S(1)}, f32[256,256]{1,0:T(8,128)S(1)}, u32[]{:S(2)}, u32[]{:S(2)}) %collective-permute-start.3) | collective-permute-done | bytes 262176 | tf_op jit(solution)/shard_map/ppermute | solution.py:21
  26.5 6.2 %convolution_bitcast_fusion = f32[32,8,32,128]{3,1,2,0:T(8,128)S(1)} fusion(f32[512,4096]{1,0:T(8,128)} %param.2, f32[256,256]{1,0:T(8,128)S(1)} %add.53, f32[256,256]{1,0:T(8,128)S(1)} %add.51), kind=kOutput, calls=%fused_computation | convolution fusion | flops 3221356544 | bytes 13107200 | tf_op jit(solution)/shard_map/dot_general | solution.py:173
  34.2 4.1 %collective-permute-done.15 = f32[4,8,128,128]{3,1,2,0:T(8,128)S(1)} collective-permute-done((f32[4,8,128,128]{3,1,2,0:T(8,128)S(1)}, f32[4,8,128,128]{3,1,2,0:T(8,128)S(1)}, u32[]{:S(2)}, u32[]{:S(2)}) %collective-permute-start.15) | collective-permute-done | bytes 2097184 | tf_op jit(solution)/shard_map/ppermute | solution.py:21
  38.3 1.7 %fusion = f32[4,8,128,128]{3,1,2,0:T(8,128)} fusion(f32[4,8,128,128]{3,1,2,0:T(8,128)S(1)} %collective-permute-done.15, f32[1,128,4,8,128]{4,3,2,1,0:T(8,128)S(1)} %get-tuple-element.6), kind=kLoop, calls=%fused_computation.3 | loop fusion | flops 524288 | bytes 6291456 | tf_op jit(solution)/shard_map/add | solution.py:177
  40.0 4.3 %all-to-all-start = ((f32[4,8,128,128]{3,1,2,0:T(8,128)}), f32[4,8,128,128]{3,1,2,0:T(8,128)S(1)}, u32[]{:S(2)}, u32[]{:S(2)}) async-start(f32[4,8,128,128]{3,1,2,0:T(8,128)} %fusion), calls=%async_computation | async-start | bytes 4194304 | tf_op jit(solution)/shard_map/all_to_all | solution.py:178
  44.3 1.0 fusion.1
  45.4 25.5 %all-to-all-done = f32[4,8,128,128]{3,1,2,0:T(8,128)S(1)} async-done(((f32[4,8,128,128]{3,1,2,0:T(8,128)}), f32[4,8,128,128]{3,1,2,0:T(8,128)S(1)}, u32[]{:S(2)}, u32[]{:S(2)}) %all-to-all-start) | async-done | bytes 2097184 | tf_op jit(solution)/shard_map/all_to_all | solution.py:178
  71.1 0.9 copy.10
  72.0 8.5 %all-to-all-start.1 = ((f32[8,128,128]{2,1,0:T(8,128)}), f32[8,128,128]{2,1,0:T(8,128)S(1)}, u32[]{:S(2)}, u32[]{:S(2)}) async-start(f32[8,128,128]{2,1,0:T(8,128)} %copy.10), calls=%async_computation.1 | async-start | bytes 1048576 | tf_op jit(solution)/shard_map/all_to_all | solution.py:179
  81.1 2.1 %collective-permute-start.6 = (f32[64,256]{1,0:T(8,128)S(1)}, f32[64,256]{1,0:T(8,128)S(1)}, u32[]{:S(2)}, u32[]{:S(2)}) collective-permute-start(f32[64,256]{1,0:T(8,128)S(1)} %fusion.11), channel_id=1, source_target_pairs={{0,128},{64,192},{128,0},{192,64},{1,129},{65,193},{129,1},{193,65... | collective-permute-start | bytes 196616 | tf_op jit(solution)/shard_map/ppermute | solution.py:21
  83.2 2.1 %collective-permute-start.7 = (f32[64,256]{1,0:T(8,128)S(1)}, f32[64,256]{1,0:T(8,128)S(1)}, u32[]{:S(2)}, u32[]{:S(2)}) collective-permute-start(f32[64,256]{1,0:T(8,128)S(1)} %fusion.11), channel_id=1, source_target_pairs={{0,192},{64,128},{128,64},{192,0},{1,193},{65,129},{129,65},{193,1... | collective-permute-start | bytes 196616 | tf_op jit(solution)/shard_map/ppermute | solution.py:21
  85.3 1.6 %collective-permute-done.6 = f32[64,256]{1,0:T(8,128)S(1)} collective-permute-done((f32[64,256]{1,0:T(8,128)S(1)}, f32[64,256]{1,0:T(8,128)S(1)}, u32[]{:S(2)}, u32[]{:S(2)}) %collective-permute-start.6) | collective-permute-done | bytes 65568 | tf_op jit(solution)/shard_map/ppermute | solution.py:21
  86.9 1.8 %collective-permute-done.7 = f32[64,256]{1,0:T(8,128)S(1)} collective-permute-done((f32[64,256]{1,0:T(8,128)S(1)}, f32[64,256]{1,0:T(8,128)S(1)}, u32[]{:S(2)}, u32[]{:S(2)}) %collective-permute-start.7) | collective-permute-done | bytes 65568 | tf_op jit(solution)/shard_map/ppermute | solution.py:21
  88.7 3.9 %collective-permute-start.10 = (f32[64,256]{1,0:T(8,128)S(1)}, f32[64,256]{1,0:T(8,128)S(1)}, u32[]{:S(2)}, u32[]{:S(2)}) collective-permute-start(f32[64,256]{1,0:T(8,128)S(1)} %add_add_fusion.1), channel_id=1, source_target_pairs={{0,24},{8,16},{16,8},{24,0},{32,56},{40,48},{48,40},{56,32},{1,25}... | collective-permute-start | bytes 196616 | tf_op jit(solution)/shard_map/ppermute | solution.py:21
  93.2 3.7 %collective-permute-done.10 = f32[64,256]{1,0:T(8,128)S(1)} collective-permute-done((f32[64,256]{1,0:T(8,128)S(1)}, f32[64,256]{1,0:T(8,128)S(1)}, u32[]{:S(2)}, u32[]{:S(2)}) %collective-permute-start.10) | collective-permute-done | bytes 65568 | tf_op jit(solution)/shard_map/ppermute | solution.py:21
  97.3 2.4 %collective-permute-done.9 = f32[64,256]{1,0:T(8,128)S(1)} collective-permute-done((f32[64,256]{1,0:T(8,128)S(1)}, f32[64,256]{1,0:T(8,128)S(1)}, u32[]{:S(2)}, u32[]{:S(2)}) %collective-permute-start.9) | collective-permute-done | bytes 65568 | tf_op jit(solution)/shard_map/ppermute | solution.py:21
  99.7 2.8 %collective-permute-start.11 = (f32[64,256]{1,0:T(8,128)S(1)}, f32[64,256]{1,0:T(8,128)S(1)}, u32[]{:S(2)}, u32[]{:S(2)}) collective-permute-start(f32[64,256]{1,0:T(8,128)S(1)} %add_add_fusion), channel_id=1, source_target_pairs={{0,56},{8,48},{16,40},{24,32},{32,24},{40,16},{48,8},{56,0},{1,57}... | collective-permute-start | bytes 196616 | tf_op jit(solution)/shard_map/ppermute | solution.py:21
  102.5 3.5 %collective-permute-done.11 = f32[64,256]{1,0:T(8,128)S(1)} collective-permute-done((f32[64,256]{1,0:T(8,128)S(1)}, f32[64,256]{1,0:T(8,128)S(1)}, u32[]{:S(2)}, u32[]{:S(2)}) %collective-permute-start.11) | collective-permute-done | bytes 65568 | tf_op jit(solution)/shard_map/ppermute | solution.py:21
  106.0 1.8 %collective-permute-start.12 = (f32[64,256]{1,0:T(8,128)S(1)}, f32[64,256]{1,0:T(8,128)S(1)}, u32[]{:S(2)}, u32[]{:S(2)}) collective-permute-start(f32[64,256]{1,0:T(8,128)S(1)} %add.62.refs_0_), channel_id=1, source_target_pairs={{0,1},{1,0},{2,3},{3,2},{4,5},{5,4},{6,7},{7,6},{8,9},{9,8},{10,11... | collective-permute-start | bytes 196616 | tf_op jit(solution)/shard_map/ppermute | solution.py:21
  108.3 1.3 collective-permute-start.14
  110.4 3.2 %collective-permute-done.13.refs_2_ = f32[64,256]{1,0:T(8,128)S(1)} collective-permute-done((f32[64,256]{1,0:T(8,128)S(1)}, f32[64,256]{1,0:T(8,128)S(1)}, u32[]{:S(2)}, u32[]{:S(2)}) %collective-permute-start.13) | collective-permute-done | bytes 65568 | tf_op jit(solution)/shard_map/ppermute | solution.py:21
  113.6 10.8 %inverse_factor.1 = (f32[256,256]{1,0:T(8,128)S(1)}, f32[2,128,256]{2,1,0:T(8,128)S(1)}) custom-call(s32[1]{0:T(128)} %bitcast.place_ref, f32[64,256]{1,0:T(8,128)S(1)} %add.62.refs_0_, f32[64,256]{1,0:T(8,128)S(1)} %collective-permute-done.12.refs_1_, f32[64,256]{1,0:T(8,128)S(1)} %collective-permute-done.13.refs_2_, ...), custom_call_target="tpu_custom_call" | custom-call | flops 3355443200 | bytes 786432 | tf_op jit(solution)/shard_map/inverse_factor/pallas_call | solution.py:102
  124.4 0.9 owned_rows.1
  125.3 6.4 %all-to-all-start.2 = ((f32[32,4,128]{2,1,0:T(4,128)}), f32[32,4,128]{2,1,0:T(4,128)S(1)}, u32[]{:S(2)}, u32[]{:S(2)}) async-start(f32[32,4,128]{2,1,0:T(4,128)} %owned_rows.1), calls=%async_computation.2 | async-start | bytes 131072 | tf_op jit(solution)/shard_map/all_to_all | solution.py:186
  131.8 1.4 convolution_multiply_fusion
  133.2 8.6 %all-to-all-done.2 = f32[32,4,128]{2,1,0:T(4,128)S(1)} async-done(((f32[32,4,128]{2,1,0:T(4,128)}), f32[32,4,128]{2,1,0:T(4,128)S(1)}, u32[]{:S(2)}, u32[]{:S(2)}) %all-to-all-start.2) | async-done | bytes 65568 | tf_op jit(solution)/shard_map/all_to_all | solution.py:186
  (31 shorter events, 7.1 us)
Async XLA Ops:
  8.1 8.1 %collective-permute-start = (f32[256,256]{1,0:T(8,128)S(1)}, f32[256,256]{1,0:T(8,128)S(1)}, u32[]{:S(2)}, u32[]{:S(2)}) collective-permute-start(f32[256,256]{1,0:T(8,128)S(1)} %get-tuple-element.10), channel_id=1, source_target_pairs={{0,1},{1,0},{2,3},{3,2},{4,5},{5,4},{6,7},{7,6},{8,9},{9,8},{10,11... | collective-permute-start | bytes 786440 | tf_op jit(solution)/shard_map/ppermute | solution.py:21
  10.4 6.7 %collective-permute-start.2 = (f32[256,256]{1,0:T(8,128)S(1)}, f32[256,256]{1,0:T(8,128)S(1)}, u32[]{:S(2)}, u32[]{:S(2)}) collective-permute-start(f32[256,256]{1,0:T(8,128)S(1)} %get-tuple-element.11), channel_id=1, source_target_pairs={{0,3},{1,2},{2,1},{3,0},{4,7},{5,6},{6,5},{7,4},{8,11},{9,10},{10,... | collective-permute-start | bytes 786440 | tf_op jit(solution)/shard_map/ppermute | solution.py:21
  17.2 7.0 %collective-permute-start.1 = (f32[256,256]{1,0:T(8,128)S(1)}, f32[256,256]{1,0:T(8,128)S(1)}, u32[]{:S(2)}, u32[]{:S(2)}) collective-permute-start(f32[256,256]{1,0:T(8,128)S(1)} %get-tuple-element.8), channel_id=1, source_target_pairs={{0,3},{1,2},{2,1},{3,0},{4,7},{5,6},{6,5},{7,4},{8,11},{9,10},{10,... | collective-permute-start | bytes 786440 | tf_op jit(solution)/shard_map/ppermute | solution.py:21
  19.0 7.4 %collective-permute-start.3 = (f32[256,256]{1,0:T(8,128)S(1)}, f32[256,256]{1,0:T(8,128)S(1)}, u32[]{:S(2)}, u32[]{:S(2)}) collective-permute-start(f32[256,256]{1,0:T(8,128)S(1)} %get-tuple-element.9), channel_id=1, source_target_pairs={{0,1},{1,0},{2,3},{3,2},{4,5},{5,4},{6,7},{7,6},{8,9},{9,8},{10,11... | collective-permute-start | bytes 786440 | tf_op jit(solution)/shard_map/ppermute | solution.py:21
  34.1 4.2 %collective-permute-start.15 = (f32[4,8,128,128]{3,1,2,0:T(8,128)S(1)}, f32[4,8,128,128]{3,1,2,0:T(8,128)S(1)}, u32[]{:S(2)}, u32[]{:S(2)}) collective-permute-start(f32[4,8,128,128]{3,1,2,0:T(8,128)S(1)} %bitcast.25), channel_id=1, source_target_pairs={{0,4},{4,0},{1,5},{5,1},{2,6},{6,2},{3,7},{7,3},{8,12},{12,8},{9,1... | collective-permute-start | bytes 6291464 | tf_op jit(solution)/shard_map/ppermute | solution.py:21
  40.0 30.9 %all-to-all-start = ((f32[4,8,128,128]{3,1,2,0:T(8,128)}), f32[4,8,128,128]{3,1,2,0:T(8,128)S(1)}, u32[]{:S(2)}, u32[]{:S(2)}) async-start(f32[4,8,128,128]{3,1,2,0:T(8,128)} %fusion), calls=%async_computation | async-start | bytes 4194304 | tf_op jit(solution)/shard_map/all_to_all | solution.py:178
  45.3 35.1 %collective-permute-start.4 = (f32[64,256]{1,0:T(8,128)S(1)}, f32[64,256]{1,0:T(8,128)S(1)}, u32[]{:S(2)}, u32[]{:S(2)}) collective-permute-start(f32[64,256]{1,0:T(8,128)S(1)} %constant_dynamic-slice_fusion.2), channel_id=1, source_target_pairs={{0,4},{4,0},{1,5},{5,1},{2,6},{6,2},{3,7},{7,3},{8,12},{12,8},{9,1... | collective-permute-start | bytes 196616 | tf_op jit(solution)/shard_map/ppermute | solution.py:21
  72.0 37.6 %all-to-all-start.1 = ((f32[8,128,128]{2,1,0:T(8,128)}), f32[8,128,128]{2,1,0:T(8,128)S(1)}, u32[]{:S(2)}, u32[]{:S(2)}) async-start(f32[8,128,128]{2,1,0:T(8,128)} %copy.10), calls=%async_computation.1 | async-start | bytes 1048576 | tf_op jit(solution)/shard_map/all_to_all | solution.py:179
  80.5 4.8 %collective-permute-start.5 = (f32[64,256]{1,0:T(8,128)S(1)}, f32[64,256]{1,0:T(8,128)S(1)}, u32[]{:S(2)}, u32[]{:S(2)}) collective-permute-start(f32[64,256]{1,0:T(8,128)S(1)} %fusion.11), channel_id=1, source_target_pairs={{0,64},{64,0},{128,192},{192,128},{1,65},{65,1},{129,193},{193,129... | collective-permute-start | bytes 196616 | tf_op jit(solution)/shard_map/ppermute | solution.py:21
  81.1 5.8 %collective-permute-start.6 = (f32[64,256]{1,0:T(8,128)S(1)}, f32[64,256]{1,0:T(8,128)S(1)}, u32[]{:S(2)}, u32[]{:S(2)}) collective-permute-start(f32[64,256]{1,0:T(8,128)S(1)} %fusion.11), channel_id=1, source_target_pairs={{0,128},{64,192},{128,0},{192,64},{1,129},{65,193},{129,1},{193,65... | collective-permute-start | bytes 196616 | tf_op jit(solution)/shard_map/ppermute | solution.py:21
  83.2 5.5 %collective-permute-start.7 = (f32[64,256]{1,0:T(8,128)S(1)}, f32[64,256]{1,0:T(8,128)S(1)}, u32[]{:S(2)}, u32[]{:S(2)}) collective-permute-start(f32[64,256]{1,0:T(8,128)S(1)} %fusion.11), channel_id=1, source_target_pairs={{0,192},{64,128},{128,64},{192,0},{1,193},{65,129},{129,65},{193,1... | collective-permute-start | bytes 196616 | tf_op jit(solution)/shard_map/ppermute | solution.py:21
  88.7 8.2 %collective-permute-start.10 = (f32[64,256]{1,0:T(8,128)S(1)}, f32[64,256]{1,0:T(8,128)S(1)}, u32[]{:S(2)}, u32[]{:S(2)}) collective-permute-start(f32[64,256]{1,0:T(8,128)S(1)} %add_add_fusion.1), channel_id=1, source_target_pairs={{0,24},{8,16},{16,8},{24,0},{32,56},{40,48},{48,40},{56,32},{1,25}... | collective-permute-start | bytes 196616 | tf_op jit(solution)/shard_map/ppermute | solution.py:21
  92.6 4.7 %collective-permute-start.8 = (f32[64,256]{1,0:T(8,128)S(1)}, f32[64,256]{1,0:T(8,128)S(1)}, u32[]{:S(2)}, u32[]{:S(2)}) collective-permute-start(f32[64,256]{1,0:T(8,128)S(1)} %add_add_fusion.1), channel_id=1, source_target_pairs={{0,8},{8,0},{16,24},{24,16},{32,40},{40,32},{48,56},{56,48},{1,9},... | collective-permute-start | bytes 196616 | tf_op jit(solution)/shard_map/ppermute | solution.py:21
  92.6 7.1 %collective-permute-start.9 = (f32[64,256]{1,0:T(8,128)S(1)}, f32[64,256]{1,0:T(8,128)S(1)}, u32[]{:S(2)}, u32[]{:S(2)}) collective-permute-start(f32[64,256]{1,0:T(8,128)S(1)} %add_add_fusion.1), channel_id=1, source_target_pairs={{0,16},{8,24},{16,0},{24,8},{32,48},{40,56},{48,32},{56,40},{1,17}... | collective-permute-start | bytes 196616 | tf_op jit(solution)/shard_map/ppermute | solution.py:21
  99.7 6.3 %collective-permute-start.11 = (f32[64,256]{1,0:T(8,128)S(1)}, f32[64,256]{1,0:T(8,128)S(1)}, u32[]{:S(2)}, u32[]{:S(2)}) collective-permute-start(f32[64,256]{1,0:T(8,128)S(1)} %add_add_fusion), channel_id=1, source_target_pairs={{0,56},{8,48},{16,40},{24,32},{32,24},{40,16},{48,8},{56,0},{1,57}... | collective-permute-start | bytes 196616 | tf_op jit(solution)/shard_map/ppermute | solution.py:21
  106.0 4.4 %collective-permute-start.12 = (f32[64,256]{1,0:T(8,128)S(1)}, f32[64,256]{1,0:T(8,128)S(1)}, u32[]{:S(2)}, u32[]{:S(2)}) collective-permute-start(f32[64,256]{1,0:T(8,128)S(1)} %add.62.refs_0_), channel_id=1, source_target_pairs={{0,1},{1,0},{2,3},{3,2},{4,5},{5,4},{6,7},{7,6},{8,9},{9,8},{10,11... | collective-permute-start | bytes 196616 | tf_op jit(solution)/shard_map/ppermute | solution.py:21
  107.8 5.8 %collective-permute-start.13 = (f32[64,256]{1,0:T(8,128)S(1)}, f32[64,256]{1,0:T(8,128)S(1)}, u32[]{:S(2)}, u32[]{:S(2)}) collective-permute-start(f32[64,256]{1,0:T(8,128)S(1)} %add.62.refs_0_), channel_id=1, source_target_pairs={{0,2},{1,3},{2,0},{3,1},{4,6},{5,7},{6,4},{7,5},{8,10},{9,11},{10,... | collective-permute-start | bytes 196616 | tf_op jit(solution)/shard_map/ppermute | solution.py:21
  108.3 5.3 %collective-permute-start.14 = (f32[64,256]{1,0:T(8,128)S(1)}, f32[64,256]{1,0:T(8,128)S(1)}, u32[]{:S(2)}, u32[]{:S(2)}) collective-permute-start(f32[64,256]{1,0:T(8,128)S(1)} %add.62.refs_0_), channel_id=1, source_target_pairs={{0,3},{1,2},{2,1},{3,0},{4,7},{5,6},{6,5},{7,4},{8,11},{9,10},{10,... | collective-permute-start | bytes 196616 | tf_op jit(solution)/shard_map/ppermute | solution.py:21
  109.6 14.8 %collective-permute-start.16 = (f32[128,128]{1,0:T(8,128)S(1)}, f32[128,128]{1,0:T(8,128)S(1)}, u32[]{:S(2)}, u32[]{:S(2)}) collective-permute-start(f32[128,128]{1,0:T(8,128)S(1)} %reduce_sum.19.mine_ref), channel_id=1, source_target_pairs={{0,4},{4,0},{1,5},{5,1},{2,6},{6,2},{3,7},{7,3},{8,12},{12,8},{9,1... | collective-permute-start | bytes 196616 | tf_op jit(solution)/shard_map/ppermute | solution.py:21
  125.3 16.5 %all-to-all-start.2 = ((f32[32,4,128]{2,1,0:T(4,128)}), f32[32,4,128]{2,1,0:T(4,128)S(1)}, u32[]{:S(2)}, u32[]{:S(2)}) async-start(f32[32,4,128]{2,1,0:T(4,128)} %owned_rows.1), calls=%async_computation.2 | async-start | bytes 131072 | tf_op jit(solution)/shard_map/all_to_all | solution.py:186
